TPU v7x, 32 devices: a whole 2x2x4 slice. The times are simulated.
32 devices in a mesh: lat: 4 (over y, x), kpt: 8 (over z, core).
Axes of the slice: x: 2, y: 2, z: 4, core: 2. Of those that a mesh axis runs over, the one named last changes fastest.
Arguments:
- coarse: bfloat16 [2, 4, 32, 12288], P(None, 'lat', 'kpt'), may hold values from -1 to 1
- rp_vectors: int32 [4, 3], P('lat'), may hold values from -4 to 4
- rp_weights: int32 [4], P('lat'), may hold values from 1 to 3
- re_vectors: int32 [32, 3], replicated, may hold values from -4 to 4
- re_weights: int32 [32], replicated, may hold values from 1 to 3
- q_points: float32 [2, 3], replicated, may hold values from 0 to 1
- k_points: float32 [512, 3], P('kpt'), may hold values from 0 to 1
- modes_rot: bfloat16 [2, 2, 48, 48], replicated, may hold values from -0.625 to 0.625
- u_k: bfloat16 [2, 512, 16, 16], P(None, 'kpt'), may hold values from -1 to 1
- u_kq: bfloat16 [2, 2, 512, 16, 16], P(None, None, 'kpt'), may hold values from -1 to 1
- mask_k: int32 [512, 16], P('kpt'), may hold values 0 or 1
- mask_kq: int32 [2, 512, 16], P(None, 'kpt'), may hold values 0 or 1
Outputs:
- coupling: bfloat16 [2, 512, 2, 12288], P(None, 'kpt', None, 'lat')
All inputs are finite; a program needn't handle non-finite values. No bound on the sum of `mask_k` or of `mask_kq` on one device may be relied on, other than what follows from the above.
Results may differ from a plain program's by a relative error of at most 0.017.
Values may be sent and summed in bfloat16 or wider, within the bound.
A program may use at most 128 MiB of HBM per device.

v0:
```python
import functools

import jax
import jax.numpy as jnp
from jax import lax
from jax.experimental import pallas as pl
from jax.experimental.pallas import tpu as pltpu
from jax.sharding import PartitionSpec as P

two_pi = 6.283185307179586
f32 = jnp.float32
bf16 = jnp.bfloat16
MESH = pl.DeviceIdType.MESH


def phases(points, vectors, weights):
    cells = vectors.astype(f32)
    argument = two_pi * (
        points[None, :, 0] * cells[:, 0:1]
        + points[None, :, 1] * cells[:, 1:2]
        + points[None, :, 2] * cells[:, 2:3]
    )
    inverse = (1.0 / weights.astype(f32))[:, None]
    return (
        (jnp.cos(argument) * inverse).astype(bf16),
        (jnp.sin(argument) * inverse).astype(bf16),
    )


def rotate_kernel(lanes, width, lat_count, kpt_count, x_ref, rot_ref, out_ref, rows_ref, branch, own_sem, lat_send, lat_recv, chip_send, chip_recv, pair_send, pair_recv):
    lat = lax.axis_index("lat")
    kpt = lax.axis_index("kpt")
    chips = kpt_count // 2
    chip = kpt // 2
    core = kpt - 2 * chip
    pair = 2 * chip + 1 - core

    def lat_peer(step):
        return lax.rem(lat + step, lat_count)

    def chip_peer(step):
        return lax.rem(chip + step, chips)

    barrier = pltpu.get_barrier_semaphore()
    for step in range(1, lat_count):
        pl.semaphore_signal(barrier, inc=1, device_id=(lat_peer(step), kpt), device_id_type=MESH)
    for step in range(1, chips):
        pl.semaphore_signal(barrier, inc=1, device_id=(lat, 2 * chip_peer(step) + core), device_id_type=MESH)
    pl.semaphore_signal(barrier, inc=1, device_id=(lat, pair), device_id_type=MESH)

    count = lanes // width
    out_rows = rows_ref.shape[0] // count
    tail = x_ref[:, lanes:].astype(f32).T[: max(8, out_rows)].astype(bf16)
    total = jnp.dot(tail, x_ref[:, :lanes], preferred_element_type=f32)
    for row in range(out_rows):
        for m in range(count):
            rows_ref[pl.ds(row * count + m, 1), :] = total[row : row + 1, m * width : (m + 1) * width]
    turned = jnp.dot(
        rot_ref[...], rows_ref[...].astype(bf16), preferred_element_type=f32
    ).astype(bf16)
    rows = branch.shape[1]
    for d in range(lat_count):
        branch[d] = turned[d * rows : (d + 1) * rows]

    pl.semaphore_wait(barrier, lat_count + chips - 1)

    def chunk(owner):
        return out_ref.at[pl.ds(owner * lat_count, lat_count)]

    first = []
    for step in range(1, lat_count):
        copy = pltpu.make_async_remote_copy(
            src_ref=branch.at[lat_peer(step)],
            dst_ref=out_ref.at[kpt * lat_count + lat],
            send_sem=lat_send.at[step],
            recv_sem=lat_recv.at[step],
            device_id=(lat_peer(step), kpt),
            device_id_type=MESH,
        )
        copy.start()
        first.append(copy)
    own = pltpu.make_async_copy(branch.at[lat], out_ref.at[kpt * lat_count + lat], own_sem)
    own.start()
    own.wait()
    for copy in first:
        copy.wait_recv()

    second = []
    for step in range(1, chips):
        copy = pltpu.make_async_remote_copy(
            src_ref=chunk(kpt),
            dst_ref=chunk(kpt),
            send_sem=chip_send.at[step],
            recv_sem=chip_recv.at[step],
            device_id=(lat, 2 * chip_peer(step) + core),
            device_id_type=MESH,
        )
        copy.start()
        second.append(copy)

    third = []
    for step in range(chips):
        source = 2 * lax.rem(chip + chips - step, chips) + core
        if step > 0:
            second[step - 1].wait_recv()
        copy = pltpu.make_async_remote_copy(
            src_ref=chunk(source),
            dst_ref=chunk(source),
            send_sem=pair_send.at[step],
            recv_sem=pair_recv.at[step],
            device_id=(lat, pair),
            device_id_type=MESH,
        )
        copy.start()
        third.append(copy)
    for copy in third:
        copy.wait_recv()
    for copy in first + second + third:
        copy.wait_send()


def couple_kernel(cells, modes, rows, bands, p_ref, kr_ref, ki_ref, u_ref, v_ref, mk_ref, mkq_ref, out_ref, wide, ph, us, vs, bs, hs, res):
    m = pl.program_id(0)
    lanes = us.shape[2]
    q_count, k_count = v_ref.shape[1], v_ref.shape[3]

    def tile(index):
        return pl.ds(pl.multiple_of(index * bands, bands), bands)

    @pl.when(m == 0)
    def _():
        for t in range(wide.shape[0]):
            wide[t] = p_ref[:, :, t * 128 : (t + 1) * 128].astype(f32).reshape(wide.shape[1:])
        row = lax.broadcasted_iota(jnp.int32, (k_count, lanes), 0)
        col = lax.broadcasted_iota(jnp.int32, (k_count, lanes), 1)
        place = [(col == row * q_count + q).astype(f32).astype(bf16) for q in range(q_count)]

        def put(value, q):
            return jnp.dot(value, place[q], preferred_element_type=f32)

        for q in range(q_count):
            re, im = put(kr_ref[...], q), put(ki_ref[...], q)
            at = 2 * q * cells
            ph[at : at + cells, :lanes] = re.astype(bf16)
            ph[at : at + cells, lanes:] = im.astype(bf16)
            ph[at + cells : at + 2 * cells, :lanes] = (-im).astype(bf16)
            ph[at + cells : at + 2 * cells, lanes:] = re.astype(bf16)
        keep = sum(put(mk_ref[...].astype(f32).astype(bf16), q) for q in range(q_count))
        keep = jnp.concatenate([keep] * bands, axis=0)
        re = sum(put(u_ref[0], q) for q in range(q_count)) * keep
        im = sum(put(u_ref[1], q) for q in range(q_count)) * keep
        us[0], us[1], us[2] = re, im - re, re + im
        keep = sum(put(mkq_ref[q].astype(f32).astype(bf16), q) for q in range(q_count))
        keep = jnp.concatenate([keep] * bands, axis=0)
        re = sum(put(v_ref[0, q], q) for q in range(q_count)) * keep
        im = -sum(put(v_ref[1, q], q) for q in range(q_count)) * keep
        vs[0], vs[1], vs[2] = re, im - re, re + im

    parts = [
        jnp.concatenate(
            [
                wide.at[t][pl.ds((2 * q + c) * modes + m, cells, stride=rows), :]
                for t in range(wide.shape[0])
            ],
            axis=1,
        )
        for q in range(q_count)
        for c in range(2)
    ]
    pair = jnp.concatenate(parts, axis=0).astype(bf16)
    field = lax.dot_general(pair, ph[...], (((0,), (0,)), ((), ())), preferred_element_type=f32)
    bs[1] = field[:, :lanes]
    bs[2] = field[:, lanes:]
    bs[0] = field[:, :lanes] + field[:, lanes:]
    group = 4

    def step_half(g, carry):
        base = g * (group * bands)
        acc = [[jnp.zeros((bands, lanes), f32)] * 3 for _ in range(group)]
        for b in range(bands):
            w = [us[t, b * bands : (b + 1) * bands, :] for t in range(3)]
            for j in range(group):
                r = base + j * bands + b
                acc[j] = [acc[j][t] + w[t] * bs[t, pl.ds(r, 1), :] for t in range(3)]
        for j in range(group):
            at = tile(g * group + j)
            re, im = acc[j][0] - acc[j][2], acc[j][0] + acc[j][1]
            hs[0, at, :], hs[1, at, :], hs[2, at, :] = re + im, re, im
        return carry

    lax.fori_loop(0, bands // group, step_half, 0)

    def step_out(g, carry):
        base = g * group
        acc = [[jnp.zeros((bands, lanes), f32)] * 3 for _ in range(group)]
        for a in range(bands):
            w = [hs[t, a * bands : (a + 1) * bands, :] for t in range(3)]
            for j in range(group):
                r = a * bands + base + j
                acc[j] = [acc[j][t] + w[t] * vs[t, pl.ds(r, 1), :] for t in range(3)]
        for j in range(group):
            at = tile(base + j)
            res[0, at, :], res[1, at, :] = acc[j][0] - acc[j][2], acc[j][0] + acc[j][1]
        return carry

    lax.fori_loop(0, bands // group, step_out, 0)
    for c in range(2):
        out_ref[c] = res[c].T.reshape(out_ref.shape[1:]).astype(bf16)


def per_device(
    lat_count,
    kpt_count,
    coarse,
    rp_vectors,
    rp_weights,
    re_vectors,
    re_weights,
    q_points,
    k_points,
    modes_rot,
    u_k,
    u_kq,
    mask_k,
    mask_kq,
):
    q_count = q_points.shape[0]
    k_count = k_points.shape[0]
    bands = u_k.shape[2]
    width = bands * bands
    lanes = coarse.shape[3]
    mode_count = lanes // width
    modes = mode_count // lat_count
    cells = re_vectors.shape[0]
    rows = 2 * q_count * modes
    assert coarse.shape[1] == 1 and coarse.shape[2] == lat_count

    pr, pi = phases(q_points, rp_vectors, rp_weights)
    tail = jnp.concatenate(
        [jnp.concatenate([pr, pi], 1), jnp.concatenate([-pi, pr], 1)], 0
    )
    tail = jnp.pad(tail, ((0, 0), (0, 128 - 2 * q_count)))
    block = jnp.transpose(coarse[:, 0], (1, 0, 2))
    sent = jnp.concatenate([block, jnp.broadcast_to(tail[None], (lat_count, 2, 128))], 2)
    got = lax.all_to_all(sent, "lat", split_axis=0, concat_axis=0, tiled=True)
    got = got.reshape(2 * lat_count, lanes + 128)

    rr, ri = modes_rot[0], modes_rot[1]
    turn = jnp.stack([jnp.stack([rr, -ri]), jnp.stack([ri, rr])])
    turn = turn.reshape(2, 2, q_count, mode_count, lat_count, modes)
    same = jnp.eye(q_count, dtype=bf16)
    turn = turn[:, :, :, :, :, :, None] * same[None, None, :, None, None, None, :]
    turn = jnp.transpose(turn, (4, 6, 0, 5, 1, 2, 3)).reshape(
        lat_count, rows, 2 * q_count * mode_count
    )
    padded = -(-rows // 16) * 16
    turn = jnp.pad(turn, ((0, 0), (0, padded - rows), (0, 0)))
    turn = turn.reshape(lat_count * padded, 2 * q_count * mode_count)
    chips = kpt_count // 2
    dma = pltpu.SemaphoreType.DMA
    portion = pl.pallas_call(
        functools.partial(rotate_kernel, lanes, width, lat_count, kpt_count),
        in_specs=[pl.BlockSpec(memory_space=pltpu.VMEM)] * 2,
        out_specs=pl.BlockSpec(memory_space=pl.ANY),
        out_shape=jax.ShapeDtypeStruct((cells, padded, width), bf16),
        scratch_shapes=[
            pltpu.VMEM((2 * q_count * mode_count, width), f32),
            pltpu.VMEM((lat_count, padded, width), bf16),
            dma,
            dma((lat_count,)),
            dma((lat_count,)),
            dma((chips,)),
            dma((chips,)),
            dma((chips,)),
            dma((chips,)),
        ],
        compiler_params=pltpu.CompilerParams(collective_id=0, has_side_effects=True),
    )(got, turn)

    kr, ki = phases(k_points, re_vectors, re_weights)
    uk = jnp.transpose(u_k, (0, 2, 3, 1)).reshape(2, width, k_count)
    ukq = jnp.transpose(u_kq, (0, 1, 3, 4, 2)).reshape(2, q_count, width, k_count)
    keep_k = jnp.transpose(mask_k)
    keep_kq = jnp.transpose(mask_kq, (0, 2, 1))

    wide_lanes = q_count * k_count
    fixed = lambda array: pl.BlockSpec(array.shape, lambda m: (0,) * array.ndim)
    return pl.pallas_call(
        functools.partial(couple_kernel, cells, modes, padded, bands),
        grid=(modes,),
        in_specs=[fixed(x) for x in (portion, kr, ki, uk, ukq, keep_k, keep_kq)],
        out_specs=pl.BlockSpec((2, k_count, q_count, width), lambda m: (0, 0, 0, m)),
        out_shape=jax.ShapeDtypeStruct((2, k_count, q_count, modes * width), bf16),
        scratch_shapes=[
            pltpu.VMEM((width // 128, cells * padded, 128), f32),
            pltpu.VMEM((2 * q_count * cells, 2 * wide_lanes), bf16),
            pltpu.VMEM((3, width, wide_lanes), f32),
            pltpu.VMEM((3, width, wide_lanes), f32),
            pltpu.VMEM((3, width, wide_lanes), f32),
            pltpu.VMEM((3, width, wide_lanes), f32),
            pltpu.VMEM((2, width, wide_lanes), f32),
        ],
    )(portion, kr, ki, uk, ukq, keep_k, keep_kq)


def solution(mesh):
    placed = (
        P(None, "lat", "kpt", None),
        P("lat", None),
        P("lat"),
        P(),
        P(),
        P(),
        P("kpt", None),
        P(),
        P(None, "kpt", None, None),
        P(None, None, "kpt", None, None),
        P("kpt", None),
        P(None, "kpt", None),
    )
    return jax.shard_map(
        functools.partial(per_device, mesh.shape["lat"], mesh.shape["kpt"]),
        mesh=mesh,
        in_specs=placed,
        out_specs=P(None, "kpt", None, "lat"),
        check_vma=False,
    )
```

profile of v0, /device:TPU:0, one launch (start us, length us, event | category | flops | bytes accessed | tf_op | source)
XLA Modules:
  0.0 57.2 jit_solution(4731937714310476676)
XLA Ops:
  0.7 0.7 %convert_element_type.54 = f32[1,3]{1,0:T(1,128)S(1)} convert(s32[1,3]{1,0:T(1,128)} %param.13) | non-fusion elementwise | flops 3 | bytes 24 | tf_op jit(solution)/shard_map/convert_element_type | solution.py:17
  1.3 0.6 %fusion.9 = (f32[1,1]{1,0:T(1,128)}, f32[1,1]{1,0:T(1,128)}, f32[1,1]{1,0:T(1,128)}) fusion(f32[1,3]{1,0:T(1,128)S(1)} %convert_element_type.54), kind=kLoop, calls=%fused_computation.32 | loop fusion | bytes 24 | tf_op jit(solution)/shard_map/slice | solution.py:19
  2.0 2.8 %fusion.5 = (bf16[2]{0:T(256)(128)(2,1)S(1)}, bf16[2]{0:T(256)(128)(2,1)S(1)}) fusion(f32[]{:T(128)} %bitcast.5, f32[]{:T(128)} %bitcast.4, f32[2,3]{1,0:T(2,128)} %param.17, f32[]{:T(128)} %bitcast.3, f32[]{:T(128)} %bitcast.2), kind=kLoop, calls=%fused_computation.19 | loop fusion | flops 20 | bytes 48 | tf_op jit(solution)/shard_map/convert_element_type | solution.py:26
  4.8 1.1 %copy.26 = bf16[2,1,4,12288]{3,0,2,1:T(2,128)(2,1)S(1)} copy(bf16[2,1,4,12288]{3,2,1,0:T(4,128)(2,1)} %param.12) | data formatting | bytes 393216 | tf_op args[0]
  5.9 0.1 fusion.7
  6.0 0.9 %pad_maximum_fusion = bf16[4,2,12416]{2,1,0:T(2,128)(2,1)} fusion(bf16[4,2,128]{2,1,0:T(2,128)(2,1)S(1)} %broadcast_in_dim.2, bf16[4,2,12288]{2,1,0:T(2,128)(2,1)S(1)} %bitcast.40), kind=kLoop, calls=%fused_computation | loop fusion | flops 397312 | bytes 397312 | tf_op jit(solution)/shard_map/concatenate | solution.py:244
  6.9 5.2 %all-to-all-start = ((bf16[4,2,12416]{2,1,0:T(2,128)(2,1)}), bf16[4,2,12416]{2,1,0:T(2,128)(2,1)S(1)}, u32[]{:S(2)}, u32[]{:S(2)}) async-start(bf16[4,2,12416]{2,1,0:T(2,128)(2,1)} %pad_maximum_fusion), calls=%async_computation | async-start | bytes 397312 | tf_op jit(solution)/shard_map/all_to_all | solution.py:245
  12.1 0.7 %convert_divide_fusion = f32[32]{0:T(128)S(1)} fusion(s32[32]{0:T(128)} %param.16), kind=kLoop, calls=%fused_computation.23 | loop fusion | flops 64 | bytes 256 | tf_op jit(solution)/shard_map/div | solution.py:23
  12.7 0.8 %slice_bitcast_fusion.5 = (f32[64]{0:T(128)S(1)}, f32[64]{0:T(128)S(1)}, f32[64]{0:T(128)S(1)}) fusion(f32[64,3]{0,1:T(4,128)} %param.18), kind=kLoop, calls=%fused_computation.29 | loop fusion | bytes 1536 | tf_op jit(solution)/shard_map/mul | solution.py:19
  13.5 0.7 %convert_element_type.59 = f32[32,3]{0,1:T(4,128)S(1)} convert(s32[32,3]{0,1:T(4,128)} %param.15) | non-fusion elementwise | flops 96 | bytes 768 | tf_op jit(solution)/shard_map/convert_element_type | solution.py:17
  14.2 0.8 %slice_negate_fusion = (bf16[1,2,48,48]{3,2,1,0:T(8,128)(2,1)S(1)}, bf16[1,2,48,48]{3,2,1,0:T(8,128)(2,1)S(1)}, bf16[1,2,48,48]{3,2,1,0:T(8,128)(2,1)S(1)}) fusion(bf16[2,2,48,48]{3,2,1,0:T(8,128)(2,1)} %param.19), kind=kLoop, calls=%fused_computation.31 | loop fusion | flops 4608 | bytes 46080 | tf_op jit(solution)/shard_map/neg | solution.py:249
  15.0 0.1 copy.20
  15.1 0.1 copy.21
  15.2 0.3 broadcast_multiply_fusion
  15.5 0.8 %mul.252.rot_ref = bf16[192,192]{1,0:T(8,128)(2,1)} reshape(bf16[4,2,2,12,2,2,48]{6,5,4,3,2,1,0:T(2,128)(2,1)S(1)} %broadcast_multiply_fusion) | data formatting | bytes 147456 | tf_op jit(solution)/shard_map/mul | solution.py:252
  16.3 0.8 %multiply_convert_fusion = (bf16[32,64]{1,0:T(8,128)(2,1)}, bf16[32,64]{1,0:T(8,128)(2,1)}) fusion(f32[32]{0:T(128)S(1)} %convert_divide_fusion, f32[32]{0:T(128)S(1)} %get-tuple-element.18, f32[64]{0:T(128)S(1)} %get-tuple-element.15, f32[32]{0:T(128)S(1)} %get-tuple-element.19, f32[64]{0:T(128)S(1)} %get-tuple-element.16, f32[32]{0:T(128)S(1)} %get-tuple-element.17, ...), kind=kLoop, calls=%fused_computation.6 | loop fusion | flops 20480 | bytes 9472 | tf_op jit(solution)/shard_map/convert_element_type | solution.py:26
  17.1 0.2 all-to-all-done
  17.3 0.8 %reshape.151.x_ref = bf16[8,12416]{1,0:T(8,128)(2,1)} reshape(bf16[4,2,12416]{2,1,0:T(2,128)(2,1)S(1)} %all-to-all-done) | data formatting | bytes 397312 | tf_op jit(solution)/shard_map/reshape | solution.py:246
  18.0 18.1 %shard_map.118.p_ref = bf16[32,48,256]{2,1,0:T(8,128)(2,1)} custom-call(bf16[8,12416]{1,0:T(8,128)(2,1)} %reshape.151.x_ref, bf16[192,192]{1,0:T(8,128)(2,1)} %mul.252.rot_ref), custom_call_target="tpu_custom_call" | custom-call | tf_op jit(solution)/shard_map/pallas_call | solution.py:261
  36.2 21.0 %shard_map.119 = bf16[2,64,2,3072]{3,2,1,0:T(2,128)(2,1)} custom-call(bf16[32,48,256]{2,1,0:T(8,128)(2,1)} %shard_map.118.p_ref, bf16[32,64]{1,0:T(8,128)(2,1)} %get-tuple-element.13.kr_ref, bf16[32,64]{1,0:T(8,128)(2,1)} %get-tuple-element.12.ki_ref, bf16[2,256,64]{2,1,0:T(8,128)(2,1)} %bitcast.44, bf16[2,2,256,64]{3,2,1,0:T(8,128)(2,1)} %bitcast.41, ...), custom_call_target="tpu_custom_call" | custom-call | tf_op jit(solution)/shard_map/pallas_call | solution.py:288
  (5 shorter events, 0.0 us)
Async XLA Ops:
  6.9 10.4 %all-to-all-start = ((bf16[4,2,12416]{2,1,0:T(2,128)(2,1)}), bf16[4,2,12416]{2,1,0:T(2,128)(2,1)S(1)}, u32[]{:S(2)}, u32[]{:S(2)}) async-start(bf16[4,2,12416]{2,1,0:T(2,128)(2,1)} %pad_maximum_fusion), calls=%async_computation | async-start | bytes 397312 | tf_op jit(solution)/shard_map/all_to_all | solution.py:245
where the time goes:
time: 57.6 us; the launch traced here: 57.2 us
  Pallas kernels  39.1 us (68%)
  other arithmetic  7.64 us (13%)
  starting transfers between devices  5.19 us (9%)
  local copies, waits for them, and re-layouts  4.28 us (7%)
  between operations  0.74 us (1%)
    pallas_call x1, Pallas kernels, per_device(): pl.pallas_call(functools.partial(couple_kernel, cells, modes, padded, ban...  21 us
    pallas_call x1, Pallas kernels, per_device(): pl.pallas_call(functools.partial(rotate_kernel, lanes, width, lat_count,...  18.1 us
    all_to_all x1, starting transfers between devices, per_device(): got = lax.all_to_all(sent, 'lat', split_axis=0, concat_axis=0, tiled=True)  5.19 us
    convert_element_type x2, other arithmetic, phases(): (jnp.sin(argument) * inverse).astype(bf16)  3.59 us
    convert_element_type x2, other arithmetic, phases(): cells = vectors.astype(f32)  1.34 us
  transfers between devices with their start and end apart: 1, of which 1 were waited for; matrix products, arithmetic and copies ran while one was open for 9% of the time, Pallas kernels for 0%

commit v1 on v0

v1 whole, which is shorter than its diff:
```python
import functools

import jax
import jax.numpy as jnp
from jax import lax
from jax.experimental import pallas as pl
from jax.experimental.pallas import tpu as pltpu
from jax.sharding import PartitionSpec as P

two_pi = 6.283185307179586
f32 = jnp.float32
bf16 = jnp.bfloat16
i32 = jnp.int32
MESH = pl.DeviceIdType.MESH
LANES = 128


def up(value, step):
    return -(-value // step) * step


def iota(shape, axis):
    return lax.broadcasted_iota(i32, shape, axis)


def dot(a, b):
    return jnp.dot(a, b, preferred_element_type=f32)


def exchange(tiles, unit):
    span = LANES // unit
    shape = next(t for t in tiles if t is not None).shape
    lane = iota(shape, 1)
    bit = 1
    while bit < span:
        shift = unit * bit
        odd = (lane & shift) != 0
        turned = list(tiles)
        for i in range(span):
            if i & bit:
                continue
            a, b = tiles[i], tiles[i | bit]
            if a is None:
                continue
            ahead = pltpu.roll(a, LANES - shift, 1)
            if b is None:
                turned[i], turned[i | bit] = a, ahead
            else:
                turned[i] = jnp.where(odd, pltpu.roll(b, shift, 1), a)
                turned[i | bit] = jnp.where(odd, b, ahead)
        tiles = turned
        bit *= 2
    return tiles


def kernel(
    lat_count,
    kpt_count,
    modes,
    rpv,
    rpw,
    qp,
    x_ref,
    rot_ref,
    rv_ref,
    rw_ref,
    kp_ref,
    u_ref,
    v_ref,
    mk_ref,
    mkq_ref,
    out_ref,
    xs,
    wre,
    wim,
    part,
    recv,
    turned,
    gath,
    p2,
    u2,
    gs,
    vb,
    rt,
    lat_send,
    lat_recv,
    chip_send,
    chip_recv,
    pair_send,
    pair_recv,
):
    lat = lax.axis_index("lat")
    kpt = lax.axis_index("kpt")
    chips = kpt_count // 2
    chip = kpt // 2
    core = kpt - 2 * chip
    pair = 2 * chip + 1 - core

    def lat_peer(step):
        return lax.rem(lat + step, lat_count)

    def chip_peer(step):
        return lax.rem(chip + step, chips)

    barrier = pltpu.get_barrier_semaphore()
    for step in range(1, lat_count):
        pl.semaphore_signal(barrier, inc=1, device_id=(lat_peer(step), kpt), device_id_type=MESH)
    for step in range(1, chips):
        pl.semaphore_signal(barrier, inc=1, device_id=(lat, 2 * chip_peer(step) + core), device_id_type=MESH)
    pl.semaphore_signal(barrier, inc=1, device_id=(lat, pair), device_id_type=MESH)

    q_count = rot_ref.shape[1]
    mode_count = rot_ref.shape[2]
    local = x_ref.shape[2]
    bands = mk_ref.shape[0]
    k_count = mk_ref.shape[1]
    width = bands * bands
    halves = width // LANES
    cells = rv_ref.shape[1]
    qn = part.shape[2] // 2
    span = LANES // bands

    if q_count * modes != qn:
        wre[...] = jnp.zeros_like(wre)
        wim[...] = jnp.zeros_like(wim)
    for q in range(q_count):
        argument = two_pi * (
            qp[q, 0] * rpv[0, 0].astype(f32)
            + qp[q, 1] * rpv[0, 1].astype(f32)
            + qp[q, 2] * rpv[0, 2].astype(f32)
        )
        argument = jnp.full((8, LANES), argument, f32)
        inverse = 1.0 / jnp.full((8, LANES), rpw[0].astype(f32), f32)
        pr = (jnp.cos(argument) * inverse).astype(bf16).astype(f32)[:1, :mode_count]
        pi = (jnp.sin(argument) * inverse).astype(bf16).astype(f32)[:1, :mode_count]
        mr = rot_ref[0, q].astype(f32).T
        mi = rot_ref[1, q].astype(f32).T
        wr = pr * mr - pi * mi
        wi = pr * mi + pi * mr
        for d in range(lat_count):
            rows = slice(d * modes, (d + 1) * modes)
            at = d * 2 * qn + q * modes
            wre[at : at + modes, :] = wr[rows]
            wim[at : at + modes, :] = -wi[rows]
            wre[at + qn : at + qn + modes, :] = wi[rows]
            wim[at + qn : at + qn + modes, :] = wr[rows]

    for c in range(2):
        x = x_ref[c, 0].astype(f32)
        for m in range(mode_count):
            for h in range(halves):
                at = (h * mode_count + m) * 2 * local + c * local
                lane = m * width + h * LANES
                xs[at : at + local, :] = x[:, lane : lane + LANES]

    def rows_of(c, e):
        return jnp.concatenate(
            [
                xs[pl.ds(h * mode_count * 2 * local + c * local + e, mode_count, stride=2 * local), :]
                for h in range(halves)
            ],
            axis=1,
        ).astype(bf16)

    left, right = wre[...].astype(bf16), wim[...].astype(bf16)
    for e in range(local):
        piece = (dot(left, rows_of(0, e)) + dot(right, rows_of(1, e))).astype(bf16)
        for d in range(lat_count):
            part[d, e] = piece[d * 2 * qn : (d + 1) * 2 * qn]

    pl.semaphore_wait(barrier, lat_count + chips - 1)
    first = []
    for step in range(1, lat_count):
        copy = pltpu.make_async_remote_copy(
            src_ref=part.at[lat_peer(step)],
            dst_ref=recv.at[lat],
            send_sem=lat_send.at[step],
            recv_sem=lat_recv.at[step],
            device_id=(lat_peer(step), kpt),
            device_id_type=MESH,
        )
        copy.start()
        first.append(copy)

    size = bands * k_count
    spread = iota((k_count, size), 1) - bands * iota((k_count, size), 0)
    spread = ((spread >= 0) & (spread < bands)).astype(f32).astype(bf16)
    eye = iota((cells, cells), 0) == iota((cells, cells), 1)

    def column(row):
        return jnp.sum(jnp.where(eye, row, 0.0), axis=1, keepdims=True)

    column_of = [column(rv_ref[i : i + 1, :].astype(f32)) for i in range(3)]
    argument = two_pi * (
        kp_ref[0:1, :] * column_of[0] + kp_ref[1:2, :] * column_of[1] + kp_ref[2:3, :] * column_of[2]
    )
    inverse = 1.0 / column(rw_ref[...].astype(f32))
    p2[0] = dot((jnp.cos(argument) * inverse).astype(bf16), spread)
    p2[1] = dot((jnp.sin(argument) * inverse).astype(bf16), spread)

    row = iota((width, size), 0)
    lane = iota((width, size), 1) & (bands - 1)
    pick = iota((bands, width), 1)
    order = iota((bands, width), 0)
    minor = (row & (bands - 1)) == lane
    major = (row // bands) == lane
    take_major = ((pick // bands) == order).astype(f32).astype(bf16)
    take_minor = ((pick & (bands - 1)) == order).astype(f32).astype(bf16)
    keep = jnp.concatenate([mk_ref[...].astype(f32)] * bands, axis=0)
    for c in range(2):
        wide = dot((u_ref[c].astype(f32) * keep).astype(bf16), spread)
        u2[c] = dot(take_major, jnp.where(minor, wide, 0.0).astype(bf16))
    blocks = gs.shape[0] // 2
    lanes = gs.shape[2]

    def grow(e, carry):
        pr, pi = p2[0, pl.ds(e, 1), :], p2[1, pl.ds(e, 1), :]
        re = (pr * u2[0] - pi * u2[1]).astype(bf16)
        im = pr * u2[1] + pi * u2[0]
        minus = (-im).astype(bf16)
        im = im.astype(bf16)
        at = pl.ds(pl.multiple_of(e * 2 * bands, bands), bands)
        below = pl.ds(pl.multiple_of(e * 2 * bands + bands, bands), bands)
        for t in range(blocks):
            cut = slice(t * lanes, (t + 1) * lanes)
            gs[t, at, :] = re[:, cut]
            gs[blocks + t, at, :] = im[:, cut]
            gs[t, below, :] = minus[:, cut]
            gs[blocks + t, below, :] = re[:, cut]
        return carry

    lax.fori_loop(0, cells, grow, 0)

    turn = []
    for q in range(q_count):
        keep = jnp.concatenate([mkq_ref[q].astype(f32)] * bands, axis=0)
        for c in range(2):
            wide = dot((v_ref[c, q].astype(f32) * keep).astype(bf16), spread)
            turn.append(dot(take_minor, jnp.where(major, wide, 0.0).astype(bf16)))
    tall = 2 * bands * span * q_count
    row = iota((tall, LANES), 0)
    place = row & (span * q_count - 1)
    same = [
        (place // q_count == iota((tall, LANES), 1) // bands) & (place % q_count == q) for q in range(q_count)
    ]
    repeat = (iota((tall, 2 * bands), 0) // (span * q_count)) == iota((tall, 2 * bands), 1)
    repeat = repeat.astype(f32).astype(bf16)
    for o in range(k_count // span):
        cut = slice(o * LANES, (o + 1) * LANES)
        for q in range(q_count):
            re, im = turn[2 * q][:, cut], turn[2 * q + 1][:, cut]
            both = [jnp.concatenate([re, -im], axis=0), jnp.concatenate([im, re], axis=0)]
            for c in range(2):
                wide = jnp.where(same[q], dot(repeat, both[c].astype(bf16)), 0.0)
                at = (q * 2 + c) * LANES
                vb[o, :, at : at + LANES] = wide.astype(bf16)

    for copy in first:
        copy.wait_recv()
    cut = span // 2
    for g in range(local // cut):
        rows = []
        for e in range(g * cut, (g + 1) * cut):
            total = part[lat, e].astype(f32)
            for step in range(1, lat_count):
                total = total + recv[lat_peer(step), e].astype(f32)
            rows += [total[:qn], total[qn:]]
        for h in range(halves):
            tiles = exchange([r[:, h * LANES : (h + 1) * LANES] for r in rows], bands)
            for a in range(span):
                turned[pl.ds(h * span + a, qn, stride=bands), :] = tiles[a]
        gath[kpt, g] = turned[...].astype(bf16)

    second = []
    for step in range(1, chips):
        copy = pltpu.make_async_remote_copy(
            src_ref=gath.at[kpt],
            dst_ref=gath.at[kpt],
            send_sem=chip_send.at[step],
            recv_sem=chip_recv.at[step],
            device_id=(lat, 2 * chip_peer(step) + core),
            device_id_type=MESH,
        )
        copy.start()
        second.append(copy)
    third = []
    for step in range(chips):
        source = 2 * lax.rem(chip + chips - step, chips) + core
        if step > 0:
            second[step - 1].wait_recv()
        copy = pltpu.make_async_remote_copy(
            src_ref=gath.at[source],
            dst_ref=gath.at[source],
            send_sem=pair_send.at[step],
            recv_sem=pair_recv.at[step],
            device_id=(lat, pair),
            device_id_type=MESH,
        )
        copy.start()
        third.append(copy)
    for copy in third:
        copy.wait_recv()

    groups = local // cut
    octets = -(-modes // span)
    near = lanes // LANES
    full = jnp.concatenate([gath[j, g] for j in range(kpt_count) for g in range(groups)], axis=1)

    def finish(t, carry):
        field = [dot(full, gs[c * blocks + t]) for c in range(2)]
        for o in range(near):
            for q in range(q_count):
                for c in range(2):
                    for s in range(octets):
                        tiles = []
                        for i in range(span):
                            m = s * span + i
                            at = (q * modes + m) * bands
                            tiles.append(
                                field[c][at : at + bands, o * LANES : (o + 1) * LANES] if m < modes else None
                            )
                        tiles = exchange(tiles, bands)
                        for i in range(span):
                            at = ((q * 2 + c) * span + i) * bands
                            rt[o, at : at + bands, s * LANES : (s + 1) * LANES] = tiles[i].astype(bf16)
            done = dot(vb[t * near + o], rt[o])
            rows = span * q_count
            for c in range(2):
                for h in range(bands // span):
                    for s in range(octets):
                        tiles = []
                        for i in range(span):
                            at = (c * bands + h * span + i) * rows
                            tiles.append(done[at : at + rows, s * LANES : (s + 1) * LANES])
                        tiles = exchange(tiles, bands)
                        for i in range(min(span, modes - s * span)):
                            at = (s * span + i) * width + h * LANES
                            k = pl.ds(pl.multiple_of((t * near + o) * span, span), span)
                            out_ref[c, k, :, at : at + LANES] = (
                                tiles[i].astype(bf16).reshape(span, q_count, LANES)
                            )
        return carry

    lax.fori_loop(0, blocks, finish, 0)
    for copy in first + second + third:
        copy.wait_send()


def per_device(
    lat_count,
    kpt_count,
    coarse,
    rp_vectors,
    rp_weights,
    re_vectors,
    re_weights,
    q_points,
    k_points,
    modes_rot,
    u_k,
    u_kq,
    mask_k,
    mask_kq,
):
    q_count = q_points.shape[0]
    k_count = k_points.shape[0]
    bands = u_k.shape[2]
    width = bands * bands
    local = coarse.shape[2]
    mode_count = coarse.shape[3] // width
    modes = mode_count // lat_count
    cells = re_vectors.shape[0]
    span = LANES // bands
    qn = up(q_count * modes, 8)
    groups = local // (span // 2)
    octets = -(-modes // span)
    chips = kpt_count // 2
    lanes = 2 * LANES
    blocks = bands * k_count // lanes
    assert coarse.shape[1] == 1 and local % (span // 2) == 0 and bands & (bands - 1) == 0

    uk = jnp.transpose(u_k, (0, 2, 3, 1)).reshape(2, width, k_count)
    ukq = jnp.transpose(u_kq, (0, 1, 3, 4, 2)).reshape(2, q_count, width, k_count)
    keep_k = jnp.transpose(mask_k)
    keep_kq = jnp.transpose(mask_kq, (0, 2, 1))

    smem = pl.BlockSpec(memory_space=pltpu.SMEM)
    vmem = pl.BlockSpec(memory_space=pltpu.VMEM)
    dma = pltpu.SemaphoreType.DMA
    tall = span * q_count * 2 * bands
    return pl.pallas_call(
        functools.partial(kernel, lat_count, kpt_count, modes),
        in_specs=[smem] * 3 + [vmem] * 9,
        out_specs=vmem,
        out_shape=jax.ShapeDtypeStruct((2, k_count, q_count, modes * width), bf16),
        scratch_shapes=[
            pltpu.VMEM((2 * local * mode_count * (width // LANES), LANES), f32),
            pltpu.VMEM((lat_count * 2 * qn, mode_count), f32),
            pltpu.VMEM((lat_count * 2 * qn, mode_count), f32),
            pltpu.VMEM((lat_count, local, 2 * qn, width), bf16),
            pltpu.VMEM((lat_count, local, 2 * qn, width), bf16),
            pltpu.VMEM((qn * bands, LANES), f32),
            pltpu.VMEM((kpt_count, groups, qn * bands, LANES), bf16),
            pltpu.VMEM((2, cells, bands * k_count), f32),
            pltpu.VMEM((2, bands, bands * k_count), f32),
            pltpu.VMEM((2 * blocks, 2 * cells * bands, lanes), bf16),
            pltpu.VMEM((k_count // span, tall, q_count * 2 * LANES), bf16),
            pltpu.VMEM((lanes // LANES, q_count * 2 * LANES, octets * LANES), bf16),
            dma((lat_count,)),
            dma((lat_count,)),
            dma((chips,)),
            dma((chips,)),
            dma((chips,)),
            dma((chips,)),
        ],
        compiler_params=pltpu.CompilerParams(collective_id=0, has_side_effects=True),
    )(
        rp_vectors,
        rp_weights,
        q_points,
        coarse,
        modes_rot,
        jnp.transpose(re_vectors),
        re_weights.reshape(1, cells),
        jnp.transpose(k_points),
        uk,
        ukq,
        keep_k,
        keep_kq,
    )


def solution(mesh):
    placed = (
        P(None, "lat", "kpt", None),
        P("lat", None),
        P("lat"),
        P(),
        P(),
        P(),
        P("kpt", None),
        P(),
        P(None, "kpt", None, None),
        P(None, None, "kpt", None, None),
        P("kpt", None),
        P(None, "kpt", None),
    )
    return jax.shard_map(
        functools.partial(per_device, mesh.shape["lat"], mesh.shape["kpt"]),
        mesh=mesh,
        in_specs=placed,
        out_specs=P(None, "kpt", None, "lat"),
        check_vma=False,
    )
```

time: 57.6 us -> 35 us (0.61)
  the two profiles are of different devices: /device:TPU:0 before, /device:TPU:1 now
where the time goes in v1:
time: 35 us; the launch traced here: 34.9 us
  Pallas kernels  30.6 us (87%)
  local copies, waits for them, and re-layouts  3.63 us (10%)
  between operations  0.66 us (2%)
    pallas_call x1, Pallas kernels, per_device(): pl.pallas_call(functools.partial(kernel, lat_count, kpt_count, modes), in...  30.6 us
    unnamed x1, local copies, waits for them, and re-layouts  3.63 us

profile of v1, /device:TPU:1, one launch (start us, length us, event | category | flops | bytes accessed | tf_op | source)
XLA Modules:
  0.0 34.9 jit_solution(7283468447567508093)
XLA Ops:
  0.7 30.6 %shard_map.118 = bf16[2,64,2,3072]{3,2,1,0:T(2,128)(2,1)} custom-call(s32[1,3]{1,0:T(1,128)} %rpv.1, s32[1]{0:T(128)S(6)} %copy.14.rpw, f32[2,3]{1,0:T(2,128)} %qp.1, bf16[2,1,4,12288]{3,2,1,0:T(4,128)(2,1)} %x_ref.1, bf16[2,2,48,48]{3,2,1,0:T(8,128)(2,1)} %rot_ref.1, s32[3,32]{1,0:T(4,128)} %bitcast.15, s32[1,32]{1,0:T(1,128)} %bitcast.17, ...), custom_call_target="tpu_custom_call" | custom-call | tf_op jit(solution)/shard_map/pallas_call | solution.py:391
  31.2 3.6 %copy.15 = bf16[2,64,2,3072]{3,2,1,0:T(2,128)(2,1)} copy(bf16[2,64,2,3072]{3,2,1,0:T(2,128)(2,1)} %shard_map.118) | data formatting | bytes 3145728

commit v2 on v1

--- a/solution.py
+++ b/solution.py
@@ -27,14 +27,14 @@
     return jnp.dot(a, b, preferred_element_type=f32)
 
 
-def exchange(tiles, unit):
-    span = LANES // unit
+def exchange(tiles, unit, axis=1):
+    span = len(tiles)
     shape = next(t for t in tiles if t is not None).shape
-    lane = iota(shape, 1)
+    place = iota(shape, axis)
     bit = 1
     while bit < span:
         shift = unit * bit
-        odd = (lane & shift) != 0
+        odd = (place & shift) != 0
         turned = list(tiles)
         for i in range(span):
             if i & bit:
@@ -42,24 +42,38 @@
             a, b = tiles[i], tiles[i | bit]
             if a is None:
                 continue
-            ahead = pltpu.roll(a, LANES - shift, 1)
+            ahead = pltpu.roll(a, shape[axis] - shift, axis)
             if b is None:
                 turned[i], turned[i | bit] = a, ahead
             else:
-                turned[i] = jnp.where(odd, pltpu.roll(b, shift, 1), a)
+                turned[i] = jnp.where(odd, pltpu.roll(b, shift, axis), a)
                 turned[i | bit] = jnp.where(odd, b, ahead)
         tiles = turned
         bit *= 2
     return tiles
 
 
-def kernel(
+def gather_kernel(
     lat_count,
     kpt_count,
     modes,
+    qp_hbm,
+    rpv_hbm,
+    rpw_hbm,
+    x_hbm,
+    rot_hbm,
+    rv_hbm,
+    rw_hbm,
+    kp_hbm,
+    u_hbm,
+    v_hbm,
+    mk_hbm,
+    mkq_hbm,
+    acc,
+    vb,
+    qp,
     rpv,
     rpw,
-    qp,
     x_ref,
     rot_ref,
     rv_ref,
@@ -69,7 +83,6 @@
     v_ref,
     mk_ref,
     mkq_ref,
-    out_ref,
     xs,
     wre,
     wim,
@@ -80,8 +93,7 @@
     p2,
     u2,
     gs,
-    vb,
-    rt,
+    loads,
     lat_send,
     lat_recv,
     chip_send,
@@ -89,6 +101,12 @@
     pair_send,
     pair_recv,
 ):
+    given = (qp_hbm, rpv_hbm, rpw_hbm, x_hbm, rot_hbm, rv_hbm, rw_hbm, kp_hbm, u_hbm, v_hbm, mk_hbm, mkq_hbm)
+    held = (qp, rpv, rpw, x_ref, rot_ref, rv_ref, rw_ref, kp_ref, u_ref, v_ref, mk_ref, mkq_ref)
+    load = []
+    for i in range(len(given)):
+        load.append(pltpu.make_async_copy(given[i], held[i], loads.at[i]))
+        load[i].start()
     lat = lax.axis_index("lat")
     kpt = lax.axis_index("kpt")
     chips = kpt_count // 2
@@ -119,20 +137,20 @@
     cells = rv_ref.shape[1]
     qn = part.shape[2] // 2
     span = LANES // bands
-
+    quad = 16 // (halves * q_count)
+
+    for copy in load[:5]:
+        copy.wait()
     if q_count * modes != qn:
         wre[...] = jnp.zeros_like(wre)
         wim[...] = jnp.zeros_like(wim)
     for q in range(q_count):
-        argument = two_pi * (
-            qp[q, 0] * rpv[0, 0].astype(f32)
-            + qp[q, 1] * rpv[0, 1].astype(f32)
-            + qp[q, 2] * rpv[0, 2].astype(f32)
-        )
-        argument = jnp.full((8, LANES), argument, f32)
-        inverse = 1.0 / jnp.full((8, LANES), rpw[0].astype(f32), f32)
-        pr = (jnp.cos(argument) * inverse).astype(bf16).astype(f32)[:1, :mode_count]
-        pi = (jnp.sin(argument) * inverse).astype(bf16).astype(f32)[:1, :mode_count]
+        term = qp[q : q + 1, :] * rpv[...].astype(f32)
+        argument = two_pi * (term[:, 0:1] + term[:, 1:2] + term[:, 2:3])
+        argument = jnp.broadcast_to(argument, (1, mode_count))
+        inverse = 1.0 / jnp.broadcast_to(rpw[...].astype(f32), (1, mode_count))
+        pr = (jnp.cos(argument) * inverse).astype(bf16).astype(f32)
+        pi = (jnp.sin(argument) * inverse).astype(bf16).astype(f32)
         mr = rot_ref[0, q].astype(f32).T
         mi = rot_ref[1, q].astype(f32).T
         wr = pr * mr - pi * mi
@@ -182,6 +200,8 @@
         copy.start()
         first.append(copy)
 
+    for copy in load[5:]:
+        copy.wait()
     size = bands * k_count
     spread = iota((k_count, size), 1) - bands * iota((k_count, size), 0)
     spread = ((spread >= 0) & (spread < bands)).astype(f32).astype(bf16)
@@ -238,13 +258,17 @@
             wide = dot((v_ref[c, q].astype(f32) * keep).astype(bf16), spread)
             turn.append(dot(take_minor, jnp.where(major, wide, 0.0).astype(bf16)))
     tall = 2 * bands * span * q_count
+    height = span // quad * halves * q_count * quad
     row = iota((tall, LANES), 0)
-    place = row & (span * q_count - 1)
-    same = [
-        (place // q_count == iota((tall, LANES), 1) // bands) & (place % q_count == q) for q in range(q_count)
-    ]
-    repeat = (iota((tall, 2 * bands), 0) // (span * q_count)) == iota((tall, 2 * bands), 1)
-    repeat = repeat.astype(f32).astype(bf16)
+    at_q = row & (q_count - 1)
+    at_k = ((row // (quad * halves * q_count)) & (span // quad - 1)) * quad + (
+        (row // (halves * q_count)) & (quad - 1)
+    )
+    same = [(at_k == iota((tall, LANES), 1) // bands) & (at_q == q) for q in range(q_count)]
+    row = iota((tall, 2 * bands), 0)
+    band = ((row // q_count) & (halves - 1)) * span + ((row // height) & (span - 1))
+    band = band + row // (tall // 2) * bands
+    repeat = (band == iota((tall, 2 * bands), 1)).astype(f32).astype(bf16)
     for o in range(k_count // span):
         cut = slice(o * LANES, (o + 1) * LANES)
         for q in range(q_count):
@@ -271,23 +295,37 @@
                 turned[pl.ds(h * span + a, qn, stride=bands), :] = tiles[a]
         gath[kpt, g] = turned[...].astype(bf16)
 
+    def apart(step, ordered):
+        found = 0
+        for z in range(chips):
+            others = sorted((o for o in range(chips) if o != z), key=lambda o: abs(o - z))
+            found = found + jnp.where(chip == z, ordered(others)[step], 0)
+        return found
+
     second = []
-    for step in range(1, chips):
+    for step in range(chips - 1):
         copy = pltpu.make_async_remote_copy(
             src_ref=gath.at[kpt],
             dst_ref=gath.at[kpt],
             send_sem=chip_send.at[step],
-            recv_sem=chip_recv.at[step],
-            device_id=(lat, 2 * chip_peer(step) + core),
+            recv_sem=chip_recv.at[chip],
+            device_id=(lat, 2 * apart(step, lambda o: o[::-1]) + core),
             device_id_type=MESH,
         )
         copy.start()
         second.append(copy)
-    third = []
-    for step in range(chips):
-        source = 2 * lax.rem(chip + chips - step, chips) + core
-        if step > 0:
-            second[step - 1].wait_recv()
+
+    def arrival(ref, source, sem):
+        return pltpu.make_async_remote_copy(
+            src_ref=ref.at[source],
+            dst_ref=ref.at[source],
+            send_sem=chip_send.at[0],
+            recv_sem=sem,
+            device_id=(lat, pair),
+            device_id_type=MESH,
+        )
+
+    def pass_on(step, source):
         copy = pltpu.make_async_remote_copy(
             src_ref=gath.at[source],
             dst_ref=gath.at[source],
@@ -297,17 +335,54 @@
             device_id_type=MESH,
         )
         copy.start()
-        third.append(copy)
-    for copy in third:
-        copy.wait_recv()
+        return copy
 
     groups = local // cut
+    deep = 2 * groups * LANES
+
+    def add(z, first_time):
+        left = jnp.concatenate([gath[2 * z + c, g] for c in range(2) for g in range(groups)], axis=1)
+        at = pl.ds(pl.multiple_of(z * deep, deep), deep)
+        for t in range(2 * blocks):
+            term = dot(left, gs[t, at, :])
+            acc[t] = term if first_time else acc[t] + term
+
+    nearest = [chip] + [apart(step, lambda o: o) for step in range(chips - 1)]
+    third = [pass_on(0, kpt)]
+    for step in range(chips):
+        if step + 1 < chips:
+            source = 2 * nearest[step + 1] + core
+        third[step].wait_recv()
+        add(nearest[step], step == 0)
+        if step + 1 < chips:
+            arrival(gath, source, chip_recv.at[nearest[step + 1]]).wait_recv()
+            third.append(pass_on(step + 1, source))
+    for copy in first + second + third:
+        copy.wait_send()
+
+
+def couple_kernel(modes, q_count, bands, acc, vb, out_ref, rt, scr, sems):
+    blocks = acc.shape[0] // 2
+    near = acc.shape[2] // LANES
+    span = LANES // bands
+    width = bands * bands
+    halves = width // LANES
     octets = -(-modes // span)
-    near = lanes // LANES
-    full = jnp.concatenate([gath[j, g] for j in range(kpt_count) for g in range(groups)], axis=1)
+    quad = 16 // (halves * q_count)
+    many = span // quad
+    k_count = near * blocks * span
+    held = modes * halves * q_count
+
+    def leave(t):
+        copies = []
+        for c in range(2):
+            rows = pl.ds(c * k_count + t * near * span, near * span)
+            copies.append(
+                pltpu.make_async_copy(scr.at[rows, :held], out_ref.at[rows], sems.at[t, c])
+            )
+        return copies
 
     def finish(t, carry):
-        field = [dot(full, gs[c * blocks + t]) for c in range(2)]
         for o in range(near):
             for q in range(q_count):
                 for c in range(2):
@@ -317,33 +392,40 @@
                             m = s * span + i
                             at = (q * modes + m) * bands
                             tiles.append(
-                                field[c][at : at + bands, o * LANES : (o + 1) * LANES] if m < modes else None
+                                acc[c * blocks + t, at : at + bands, o * LANES : (o + 1) * LANES].astype(bf16)
+                                if m < modes
+                                else None
                             )
                         tiles = exchange(tiles, bands)
                         for i in range(span):
                             at = ((q * 2 + c) * span + i) * bands
-                            rt[o, at : at + bands, s * LANES : (s + 1) * LANES] = tiles[i].astype(bf16)
+                            rt[o, at : at + bands, s * LANES : (s + 1) * LANES] = tiles[i]
             done = dot(vb[t * near + o], rt[o])
-            rows = span * q_count
             for c in range(2):
-                for h in range(bands // span):
+                for g in range(many):
+                    found = []
                     for s in range(octets):
                         tiles = []
                         for i in range(span):
-                            at = (c * bands + h * span + i) * rows
-                            tiles.append(done[at : at + rows, s * LANES : (s + 1) * LANES])
-                        tiles = exchange(tiles, bands)
-                        for i in range(min(span, modes - s * span)):
-                            at = (s * span + i) * width + h * LANES
-                            k = pl.ds(pl.multiple_of((t * near + o) * span, span), span)
-                            out_ref[c, k, :, at : at + LANES] = (
-                                tiles[i].astype(bf16).reshape(span, q_count, LANES)
-                            )
+                            at = ((c * span + i) * many + g) * 16
+                            tiles.append(done[at : at + 16, s * LANES : (s + 1) * LANES].astype(bf16))
+                        found += exchange(tiles, bands)
+                    for m in range(0, modes, quad):
+                        tiles = [found[i] if i < modes else None for i in range(m, m + quad)]
+                        tiles = exchange(tiles, halves * q_count, 0)
+                        tall = min(quad, modes - m) * halves * q_count
+                        for i in range(quad):
+                            k = (t * near + o) * span + g * quad + i
+                            at = m * halves * q_count
+                            scr[c * k_count + k, at : at + tall, :] = tiles[i][:tall]
+        for copy in leave(t):
+            copy.start()
         return carry
 
     lax.fori_loop(0, blocks, finish, 0)
-    for copy in first + second + third:
-        copy.wait_send()
+    for t in range(blocks):
+        for copy in leave(t):
+            copy.wait()
 
 
 def per_device(
@@ -384,40 +466,15 @@
     keep_k = jnp.transpose(mask_k)
     keep_kq = jnp.transpose(mask_kq, (0, 2, 1))
 
-    smem = pl.BlockSpec(memory_space=pltpu.SMEM)
+    anywhere = pl.BlockSpec(memory_space=pl.ANY)
     vmem = pl.BlockSpec(memory_space=pltpu.VMEM)
     dma = pltpu.SemaphoreType.DMA
     tall = span * q_count * 2 * bands
-    return pl.pallas_call(
-        functools.partial(kernel, lat_count, kpt_count, modes),
-        in_specs=[smem] * 3 + [vmem] * 9,
-        out_specs=vmem,
-        out_shape=jax.ShapeDtypeStruct((2, k_count, q_count, modes * width), bf16),
-        scratch_shapes=[
-            pltpu.VMEM((2 * local * mode_count * (width // LANES), LANES), f32),
-            pltpu.VMEM((lat_count * 2 * qn, mode_count), f32),
-            pltpu.VMEM((lat_count * 2 * qn, mode_count), f32),
-            pltpu.VMEM((lat_count, local, 2 * qn, width), bf16),
-            pltpu.VMEM((lat_count, local, 2 * qn, width), bf16),
-            pltpu.VMEM((qn * bands, LANES), f32),
-            pltpu.VMEM((kpt_count, groups, qn * bands, LANES), bf16),
-            pltpu.VMEM((2, cells, bands * k_count), f32),
-            pltpu.VMEM((2, bands, bands * k_count), f32),
-            pltpu.VMEM((2 * blocks, 2 * cells * bands, lanes), bf16),
-            pltpu.VMEM((k_count // span, tall, q_count * 2 * LANES), bf16),
-            pltpu.VMEM((lanes // LANES, q_count * 2 * LANES, octets * LANES), bf16),
-            dma((lat_count,)),
-            dma((lat_count,)),
-            dma((chips,)),
-            dma((chips,)),
-            dma((chips,)),
-            dma((chips,)),
-        ],
-        compiler_params=pltpu.CompilerParams(collective_id=0, has_side_effects=True),
-    )(
+    rows = qn * bands
+    inputs = (
+        q_points,
         rp_vectors,
-        rp_weights,
-        q_points,
+        rp_weights.reshape(1, 1),
         coarse,
         modes_rot,
         jnp.transpose(re_vectors),
@@ -428,6 +485,55 @@
         keep_k,
         keep_kq,
     )
+    acc, vb = pl.pallas_call(
+        functools.partial(gather_kernel, lat_count, kpt_count, modes),
+        in_specs=[anywhere] * len(inputs),
+        out_specs=[vmem] * 2,
+        out_shape=[
+            pltpu.VMEM((2 * blocks, rows, lanes), f32),
+            pltpu.VMEM((k_count // span, tall, q_count * 2 * LANES), bf16),
+        ],
+        scratch_shapes=[pltpu.VMEM(x.shape, x.dtype) for x in inputs]
+        + [
+            pltpu.VMEM((2 * local * mode_count * (width // LANES), LANES), f32),
+            pltpu.VMEM((lat_count * 2 * qn, mode_count), f32),
+            pltpu.VMEM((lat_count * 2 * qn, mode_count), f32),
+            pltpu.VMEM((lat_count, local, 2 * qn, width), bf16),
+            pltpu.VMEM((lat_count, local, 2 * qn, width), bf16),
+            pltpu.VMEM((rows, LANES), f32),
+            pltpu.VMEM((kpt_count, groups, rows, LANES), bf16),
+            pltpu.VMEM((2, cells, bands * k_count), f32),
+            pltpu.VMEM((2, bands, bands * k_count), f32),
+            pltpu.VMEM((2 * blocks, 2 * cells * bands, lanes), bf16),
+            dma((len(inputs),)),
+            dma((lat_count,)),
+            dma((lat_count,)),
+            dma((chips,)),
+            dma((chips,)),
+            dma((chips,)),
+            dma((chips,)),
+        ],
+        compiler_params=pltpu.CompilerParams(
+            collective_id=0, has_side_effects=True, vmem_limit_bytes=48 * 1024 * 1024
+        ),
+    )(*inputs)
+    count = modes * (width // LANES)
+    held = count * q_count
+    result = jax.ShapeDtypeStruct((2 * k_count, held, LANES), bf16)
+    out = pl.pallas_call(
+        functools.partial(couple_kernel, modes, q_count, bands),
+        in_specs=[vmem] * 2,
+        out_specs=anywhere,
+        out_shape=result,
+        scratch_shapes=[
+            pltpu.VMEM((lanes // LANES, q_count * 2 * LANES, octets * LANES), bf16),
+            pltpu.VMEM((2 * k_count, up(held, 16), LANES), bf16),
+            dma((blocks, 2)),
+        ],
+        compiler_params=pltpu.CompilerParams(vmem_limit_bytes=16 * 1024 * 1024),
+    )(acc, vb)
+    out = out.reshape(2, k_count, count, q_count, LANES)
+    return jnp.transpose(out, (0, 1, 3, 2, 4)).reshape(2, k_count, q_count, modes * width)
 
 
 def solution(mesh):

time: 35 us -> 30.2 us (0.86)
  the two profiles are of different devices: /device:TPU:1 before, /device:TPU:0 now
where the time goes in v2:
time: 30.2 us; the launch traced here: 29.9 us
  Pallas kernels  29.2 us (97%)
  between operations  0.66 us (2%)
    pallas_call x1, Pallas kernels, per_device(): pl.pallas_call(functools.partial(gather_kernel, lat_count, kpt_count, mod...  23.3 us
    pallas_call x1, Pallas kernels, per_device(): pl.pallas_call(functools.partial(couple_kernel, modes, q_count, bands), i...  5.9 us

profile of v2, /device:TPU:0, one launch (start us, length us, event | category | flops | bytes accessed | tf_op | source)
XLA Modules:
  0.0 29.9 jit_solution(8354202754770829250)
XLA Ops:
  0.7 23.3 %shard_map.118 = (f32[8,384,256]{2,1,0:T(8,128)S(1)}, bf16[8,512,512]{2,1,0:T(8,128)(2,1)S(1)}) custom-call(f32[2,3]{1,0:T(2,128)} %qp_hbm.1, s32[1,3]{1,0:T(1,128)} %rpv_hbm.1, s32[1,1]{1,0:T(1,128)} %bitcast.17.rpw_hbm, bf16[2,1,4,12288]{3,2,1,0:T(4,128)(2,1)} %x_hbm.1, bf16[2,2,48,48]{3,2,1,0:T(8,128)(2,1)} %rot_hbm.1, s32[3,32]{1,0:T(4,128)} %bitcast.22, ...), custom_call_target="tpu_custom_call" | custom-call | tf_op jit(solution)/shard_map/pallas_call | solution.py:488
  24.0 5.9 %shard_map.119 = bf16[128,48,128]{2,1,0:T(8,128)(2,1)} custom-call(f32[8,384,256]{2,1,0:T(8,128)S(1)} %get-tuple-element.7.acc, bf16[8,512,512]{2,1,0:T(8,128)(2,1)S(1)} %get-tuple-element.8.vb), custom_call_target="tpu_custom_call" | custom-call | tf_op jit(solution)/shard_map/pallas_call | solution.py:523

commit v3 on v2

--- a/solution.py
+++ b/solution.py
@@ -31,26 +31,18 @@
     span = len(tiles)
     shape = next(t for t in tiles if t is not None).shape
     place = iota(shape, axis)
+    skew = [t if i == 0 or t is None else pltpu.roll(t, i * unit, axis) for i, t in enumerate(tiles)]
+    tiles = [skew[-i % span] for i in range(span)]
     bit = 1
     while bit < span:
-        shift = unit * bit
-        odd = (place & shift) != 0
-        turned = list(tiles)
+        odd = (place & (unit * bit)) != 0
+        turned = []
         for i in range(span):
-            if i & bit:
-                continue
-            a, b = tiles[i], tiles[i | bit]
-            if a is None:
-                continue
-            ahead = pltpu.roll(a, shape[axis] - shift, axis)
-            if b is None:
-                turned[i], turned[i | bit] = a, ahead
-            else:
-                turned[i] = jnp.where(odd, pltpu.roll(b, shift, axis), a)
-                turned[i | bit] = jnp.where(odd, b, ahead)
+            a, b = tiles[i], tiles[(i - bit) % span]
+            turned.append(b if a is None else a if b is None else jnp.where(odd, b, a))
         tiles = turned
         bit *= 2
-    return tiles
+    return [t if i == 0 else pltpu.roll(t, shape[axis] - i * unit, axis) for i, t in enumerate(tiles)]
 
 
 def gather_kernel(
@@ -69,7 +61,8 @@
     v_hbm,
     mk_hbm,
     mkq_hbm,
-    acc,
+    gath,
+    gs,
     vb,
     qp,
     rpv,
@@ -89,15 +82,14 @@
     part,
     recv,
     turned,
-    gath,
     p2,
     u2,
-    gs,
     loads,
     lat_send,
     lat_recv,
     chip_send,
     chip_recv,
+    relay_send,
     pair_send,
     pair_recv,
 ):
@@ -135,7 +127,8 @@
     width = bands * bands
     halves = width // LANES
     cells = rv_ref.shape[1]
-    qn = part.shape[2] // 2
+    sets = part.shape[0]
+    qn = sets * 8
     span = LANES // bands
     quad = 16 // (halves * q_count)
 
@@ -156,12 +149,17 @@
         wr = pr * mr - pi * mi
         wi = pr * mi + pi * mr
         for d in range(lat_count):
-            rows = slice(d * modes, (d + 1) * modes)
-            at = d * 2 * qn + q * modes
-            wre[at : at + modes, :] = wr[rows]
-            wim[at : at + modes, :] = -wi[rows]
-            wre[at + qn : at + qn + modes, :] = wi[rows]
-            wim[at + qn : at + qn + modes, :] = wr[rows]
+            done = 0
+            while done < modes:
+                first_row = q * modes + done
+                take = min(8 - first_row % 8, modes - done)
+                rows = slice(d * modes + done, d * modes + done + take)
+                at = d * 2 * qn + first_row // 8 * 16 + first_row % 8
+                wre[at : at + take, :] = wr[rows]
+                wim[at : at + take, :] = -wi[rows]
+                wre[at + 8 : at + 8 + take, :] = wi[rows]
+                wim[at + 8 : at + 8 + take, :] = wr[rows]
+                done += take
 
     for c in range(2):
         x = x_ref[c, 0].astype(f32)
@@ -184,21 +182,28 @@
     for e in range(local):
         piece = (dot(left, rows_of(0, e)) + dot(right, rows_of(1, e))).astype(bf16)
         for d in range(lat_count):
-            part[d, e] = piece[d * 2 * qn : (d + 1) * 2 * qn]
+            for i in range(sets):
+                at = d * 2 * qn + i * 16
+                part[i, d, e] = piece[at : at + 16]
 
     pl.semaphore_wait(barrier, lat_count + chips - 1)
-    first = []
-    for step in range(1, lat_count):
-        copy = pltpu.make_async_remote_copy(
-            src_ref=part.at[lat_peer(step)],
-            dst_ref=recv.at[lat],
-            send_sem=lat_send.at[step],
-            recv_sem=lat_recv.at[step],
-            device_id=(lat_peer(step), kpt),
-            device_id_type=MESH,
-        )
-        copy.start()
-        first.append(copy)
+    first = [
+        [
+            pltpu.make_async_remote_copy(
+                src_ref=part.at[i, lat_peer(step)],
+                dst_ref=recv.at[i, lat],
+                send_sem=lat_send.at[i, step],
+                recv_sem=lat_recv.at[i, step],
+                device_id=(lat_peer(step), kpt),
+                device_id_type=MESH,
+            )
+            for step in range(1, lat_count)
+        ]
+        for i in range(sets)
+    ]
+    for copies in first:
+        for copy in copies:
+            copy.start()
 
     for copy in load[5:]:
         copy.wait()
@@ -251,12 +256,6 @@
 
     lax.fori_loop(0, cells, grow, 0)
 
-    turn = []
-    for q in range(q_count):
-        keep = jnp.concatenate([mkq_ref[q].astype(f32)] * bands, axis=0)
-        for c in range(2):
-            wide = dot((v_ref[c, q].astype(f32) * keep).astype(bf16), spread)
-            turn.append(dot(take_minor, jnp.where(major, wide, 0.0).astype(bf16)))
     tall = 2 * bands * span * q_count
     height = span // quad * halves * q_count * quad
     row = iota((tall, LANES), 0)
@@ -269,101 +268,125 @@
     band = ((row // q_count) & (halves - 1)) * span + ((row // height) & (span - 1))
     band = band + row // (tall // 2) * bands
     repeat = (band == iota((tall, 2 * bands), 1)).astype(f32).astype(bf16)
-    for o in range(k_count // span):
-        cut = slice(o * LANES, (o + 1) * LANES)
-        for q in range(q_count):
-            re, im = turn[2 * q][:, cut], turn[2 * q + 1][:, cut]
+
+    def lay(q):
+        keep = jnp.concatenate([mkq_ref[q].astype(f32)] * bands, axis=0)
+        turn = []
+        for c in range(2):
+            wide = dot((v_ref[c, q].astype(f32) * keep).astype(bf16), spread)
+            turn.append(dot(take_minor, jnp.where(major, wide, 0.0).astype(bf16)))
+        for o in range(k_count // span):
+            re, im = (x[:, o * LANES : (o + 1) * LANES] for x in turn)
             both = [jnp.concatenate([re, -im], axis=0), jnp.concatenate([im, re], axis=0)]
             for c in range(2):
                 wide = jnp.where(same[q], dot(repeat, both[c].astype(bf16)), 0.0)
                 at = (q * 2 + c) * LANES
                 vb[o, :, at : at + LANES] = wide.astype(bf16)
 
-    for copy in first:
-        copy.wait_recv()
-    cut = span // 2
-    for g in range(local // cut):
-        rows = []
-        for e in range(g * cut, (g + 1) * cut):
-            total = part[lat, e].astype(f32)
-            for step in range(1, lat_count):
-                total = total + recv[lat_peer(step), e].astype(f32)
-            rows += [total[:qn], total[qn:]]
-        for h in range(halves):
-            tiles = exchange([r[:, h * LANES : (h + 1) * LANES] for r in rows], bands)
-            for a in range(span):
-                turned[pl.ds(h * span + a, qn, stride=bands), :] = tiles[a]
-        gath[kpt, g] = turned[...].astype(bf16)
-
-    def apart(step, ordered):
+    def relayed(source, target):
+        if chips < 3:
+            return False
+        return ((target == chips - 1) & (source == chips - 3)) | ((target == 0) & (source == 2))
+
+    def apart(step):
         found = 0
         for z in range(chips):
-            others = sorted((o for o in range(chips) if o != z), key=lambda o: abs(o - z))
-            found = found + jnp.where(chip == z, ordered(others)[step], 0)
+            others = [o for o in range(chips) if o != z]
+            between = {1: 2, chips - 2: chips - 3}.get(z) if chips > 2 else None
+            others = sorted(others, key=lambda o: (abs(o - z), o != between))
+            found = found + jnp.where(chip == z, others[step], 0)
         return found
 
-    second = []
-    for step in range(chips - 1):
-        copy = pltpu.make_async_remote_copy(
-            src_ref=gath.at[kpt],
-            dst_ref=gath.at[kpt],
-            send_sem=chip_send.at[step],
-            recv_sem=chip_recv.at[chip],
-            device_id=(lat, 2 * apart(step, lambda o: o[::-1]) + core),
+    def over(source, i, target, send_sem, recv_sem):
+        return pltpu.make_async_remote_copy(
+            src_ref=gath.at[source, i],
+            dst_ref=gath.at[source, i],
+            send_sem=send_sem,
+            recv_sem=recv_sem,
+            device_id=(lat, target),
             device_id_type=MESH,
         )
+
+    def outward(i, act):
+        for down in (True, False):
+            for z in reversed(range(chips)) if down else range(chips):
+                ahead = (chip < z) if down else (chip > z)
+
+                @pl.when(ahead & jnp.logical_not(relayed(chip, z)))
+                def _():
+                    act(over(kpt, i, 2 * z + core, chip_send.at[i, z], chip_recv.at[i, chip]))
+
+    def onward(i, source, act):
+        for n, (at, end, origin) in enumerate(((chips - 2, chips - 1, chips - 3), (1, 0, 2))):
+            if chips < 3:
+                continue
+
+            @pl.when((chip == at) & (source == origin))
+            def _():
+                act(over(2 * source + core, i, 2 * end + core, relay_send.at[i, n], chip_recv.at[i, source]))
+
+    def start(copy):
         copy.start()
-        second.append(copy)
-
-    def arrival(ref, source, sem):
-        return pltpu.make_async_remote_copy(
-            src_ref=ref.at[source],
-            dst_ref=ref.at[source],
-            send_sem=chip_send.at[0],
-            recv_sem=sem,
-            device_id=(lat, pair),
-            device_id_type=MESH,
-        )
-
-    def pass_on(step, source):
-        copy = pltpu.make_async_remote_copy(
-            src_ref=gath.at[source],
-            dst_ref=gath.at[source],
-            send_sem=pair_send.at[step],
-            recv_sem=pair_recv.at[step],
-            device_id=(lat, pair),
-            device_id_type=MESH,
-        )
+
+    def sent(copy):
+        copy.wait_send()
+
+    third = []
+
+    def pass_on(source, i, step):
+        copy = over(source, i, pair, pair_send.at[i, step], pair_recv.at[i, step])
         copy.start()
-        return copy
-
-    groups = local // cut
-    deep = 2 * groups * LANES
-
-    def add(z, first_time):
-        left = jnp.concatenate([gath[2 * z + c, g] for c in range(2) for g in range(groups)], axis=1)
-        at = pl.ds(pl.multiple_of(z * deep, deep), deep)
-        for t in range(2 * blocks):
-            term = dot(left, gs[t, at, :])
-            acc[t] = term if first_time else acc[t] + term
-
-    nearest = [chip] + [apart(step, lambda o: o) for step in range(chips - 1)]
-    third = [pass_on(0, kpt)]
-    for step in range(chips):
-        if step + 1 < chips:
-            source = 2 * nearest[step + 1] + core
-        third[step].wait_recv()
-        add(nearest[step], step == 0)
-        if step + 1 < chips:
-            arrival(gath, source, chip_recv.at[nearest[step + 1]]).wait_recv()
-            third.append(pass_on(step + 1, source))
-    for copy in first + second + third:
+        third.append(copy)
+
+    cut = span // 2
+    for i in range(sets):
+        for copy in first[i]:
+            copy.wait_recv()
+        for g in range(local // cut):
+            rows = []
+            for e in range(g * cut, (g + 1) * cut):
+                total = part[i, lat, e].astype(f32)
+                for step in range(1, lat_count):
+                    total = total + recv[i, lat_peer(step), e].astype(f32)
+                rows += [total[:8], total[8:]]
+            for h in range(halves):
+                tiles = exchange([r[:, h * LANES : (h + 1) * LANES] for r in rows], bands)
+                for a in range(span):
+                    turned[pl.ds(h * span + a, 8, stride=bands), :] = tiles[a]
+            gath[kpt, i, g] = turned[...].astype(bf16)
+        outward(i, start)
+        pass_on(kpt, i, chips - 1)
+
+    waits = sorted(
+        ((i + min(step, 1) + 0.1 * step, step, i) for step in range(chips - 1) for i in range(sets))
+    )
+    laid = 0
+    for _, step, i in waits:
+        source = apart(step)
+        over(2 * source + core, i, pair, chip_send.at[i, 0], chip_recv.at[i, source]).wait_recv()
+        onward(i, source, start)
+        pass_on(2 * source + core, i, step)
+        if i == 0 and step != 1 and laid < q_count:
+            lay(laid)
+            laid += 1
+    for q in range(laid, q_count):
+        lay(q)
+    for copy in third:
+        copy.wait_recv()
+    for copies in first:
+        for copy in copies:
+            copy.wait_send()
+    for copy in third:
         copy.wait_send()
-
-
-def couple_kernel(modes, q_count, bands, acc, vb, out_ref, rt, scr, sems):
-    blocks = acc.shape[0] // 2
-    near = acc.shape[2] // LANES
+    for i in range(sets):
+        outward(i, sent)
+        for step in range(chips - 1):
+            onward(i, apart(step), sent)
+
+
+def couple_kernel(modes, q_count, bands, gath, gs, vb, out_ref, rt, scr, sems):
+    blocks = gs.shape[0] // 2
+    near = gs.shape[2] // LANES
     span = LANES // bands
     width = bands * bands
     halves = width // LANES
@@ -383,6 +406,15 @@
         return copies
 
     def finish(t, carry):
+        chunks, sets, groups = gath.shape[:3]
+        left = jnp.concatenate(
+            [
+                jnp.concatenate([gath[j, i, g] for j in range(chunks) for g in range(groups)], axis=1)
+                for i in range(sets)
+            ],
+            axis=0,
+        )
+        field = [dot(left, gs[c * blocks + t]).astype(bf16) for c in range(2)]
         for o in range(near):
             for q in range(q_count):
                 for c in range(2):
@@ -392,15 +424,14 @@
                             m = s * span + i
                             at = (q * modes + m) * bands
                             tiles.append(
-                                acc[c * blocks + t, at : at + bands, o * LANES : (o + 1) * LANES].astype(bf16)
-                                if m < modes
-                                else None
+                                field[c][at : at + bands, o * LANES : (o + 1) * LANES] if m < modes else None
                             )
                         tiles = exchange(tiles, bands)
                         for i in range(span):
                             at = ((q * 2 + c) * span + i) * bands
-                            rt[o, at : at + bands, s * LANES : (s + 1) * LANES] = tiles[i]
-            done = dot(vb[t * near + o], rt[o])
+                            rt[o, s, at : at + bands, :] = tiles[i]
+            right = jnp.concatenate([rt[o, s] for s in range(octets)], axis=1)
+            done = dot(vb[t * near + o], right)
             for c in range(2):
                 for g in range(many):
                     found = []
@@ -454,6 +485,7 @@
     cells = re_vectors.shape[0]
     span = LANES // bands
     qn = up(q_count * modes, 8)
+    sets = qn // 8
     groups = local // (span // 2)
     octets = -(-modes // span)
     chips = kpt_count // 2
@@ -466,11 +498,10 @@
     keep_k = jnp.transpose(mask_k)
     keep_kq = jnp.transpose(mask_kq, (0, 2, 1))
 
-    anywhere = pl.BlockSpec(memory_space=pl.ANY)
+    anywhere = pl.BlockSpec(memory_space=pltpu.HBM)
     vmem = pl.BlockSpec(memory_space=pltpu.VMEM)
     dma = pltpu.SemaphoreType.DMA
     tall = span * q_count * 2 * bands
-    rows = qn * bands
     inputs = (
         q_points,
         rp_vectors,
@@ -485,12 +516,18 @@
         keep_k,
         keep_kq,
     )
-    acc, vb = pl.pallas_call(
+    kept = (
+        2 * kpt_count * sets * groups * 8 * bands * LANES
+        + 2 * 2 * blocks * 2 * cells * bands * lanes
+        + 2 * (k_count // span) * tall * q_count * 2 * LANES
+    )
+    parts = pl.pallas_call(
         functools.partial(gather_kernel, lat_count, kpt_count, modes),
         in_specs=[anywhere] * len(inputs),
-        out_specs=[vmem] * 2,
+        out_specs=[vmem] * 3,
         out_shape=[
-            pltpu.VMEM((2 * blocks, rows, lanes), f32),
+            pltpu.VMEM((kpt_count, sets, groups, 8 * bands, LANES), bf16),
+            pltpu.VMEM((2 * blocks, 2 * cells * bands, lanes), bf16),
             pltpu.VMEM((k_count // span, tall, q_count * 2 * LANES), bf16),
         ],
         scratch_shapes=[pltpu.VMEM(x.shape, x.dtype) for x in inputs]
@@ -498,23 +535,22 @@
             pltpu.VMEM((2 * local * mode_count * (width // LANES), LANES), f32),
             pltpu.VMEM((lat_count * 2 * qn, mode_count), f32),
             pltpu.VMEM((lat_count * 2 * qn, mode_count), f32),
-            pltpu.VMEM((lat_count, local, 2 * qn, width), bf16),
-            pltpu.VMEM((lat_count, local, 2 * qn, width), bf16),
-            pltpu.VMEM((rows, LANES), f32),
-            pltpu.VMEM((kpt_count, groups, rows, LANES), bf16),
+            pltpu.VMEM((sets, lat_count, local, 16, width), bf16),
+            pltpu.VMEM((sets, lat_count, local, 16, width), bf16),
+            pltpu.VMEM((8 * bands, LANES), f32),
             pltpu.VMEM((2, cells, bands * k_count), f32),
             pltpu.VMEM((2, bands, bands * k_count), f32),
-            pltpu.VMEM((2 * blocks, 2 * cells * bands, lanes), bf16),
             dma((len(inputs),)),
-            dma((lat_count,)),
-            dma((lat_count,)),
-            dma((chips,)),
-            dma((chips,)),
-            dma((chips,)),
-            dma((chips,)),
+            dma((sets, lat_count)),
+            dma((sets, lat_count)),
+            dma((sets, chips)),
+            dma((sets, chips)),
+            dma((sets, 2)),
+            dma((sets, chips)),
+            dma((sets, chips)),
         ],
         compiler_params=pltpu.CompilerParams(
-            collective_id=0, has_side_effects=True, vmem_limit_bytes=48 * 1024 * 1024
+            collective_id=0, has_side_effects=True, vmem_limit_bytes=63 * 1024 * 1024 - kept
         ),
     )(*inputs)
     count = modes * (width // LANES)
@@ -522,16 +558,16 @@
     result = jax.ShapeDtypeStruct((2 * k_count, held, LANES), bf16)
     out = pl.pallas_call(
         functools.partial(couple_kernel, modes, q_count, bands),
-        in_specs=[vmem] * 2,
+        in_specs=[vmem] * 3,
         out_specs=anywhere,
         out_shape=result,
         scratch_shapes=[
-            pltpu.VMEM((lanes // LANES, q_count * 2 * LANES, octets * LANES), bf16),
+            pltpu.VMEM((lanes // LANES, octets, q_count * 2 * LANES, LANES), bf16),
             pltpu.VMEM((2 * k_count, up(held, 16), LANES), bf16),
             dma((blocks, 2)),
         ],
-        compiler_params=pltpu.CompilerParams(vmem_limit_bytes=16 * 1024 * 1024),
-    )(acc, vb)
+        compiler_params=pltpu.CompilerParams(vmem_limit_bytes=40 * 1024 * 1024),
+    )(*parts)
     out = out.reshape(2, k_count, count, q_count, LANES)
     return jnp.transpose(out, (0, 1, 3, 2, 4)).reshape(2, k_count, q_count, modes * width)
 

time: 30.2 us -> 28.8 us (0.954)
  Pallas kernels: 29.2 us -> 28 us
    pallas_call x1, Pallas kernels: 23.3 us -> 21.8 us  [per_device(): pl.pallas_call(functools.partial(gather_kernel, lat_count, kpt_count, mod...]
    pallas_call x1, Pallas kernels: 5.9 us -> 6.27 us  [per_device(): pl.pallas_call(functools.partial(couple_kernel, modes, q_count, bands), i...]
where the time goes in v3:
time: 28.8 us; the launch traced here: 28.7 us
  Pallas kernels  28 us (97%)
  between operations  0.66 us (2%)
    pallas_call x1, Pallas kernels, per_device(): pl.pallas_call(functools.partial(gather_kernel, lat_count, kpt_count, mod...  21.8 us
    pallas_call x1, Pallas kernels, per_device(): pl.pallas_call(functools.partial(couple_kernel, modes, q_count, bands), i...  6.27 us

profile of v3, /device:TPU:0, one launch (start us, length us, event | category | flops | bytes accessed | tf_op | source)
XLA Modules:
  0.0 28.7 jit_solution(1931487569070953933)
XLA Ops:
  0.7 21.8 %shard_map.118 = (bf16[8,3,1,128,128]{4,3,2,1,0:T(8,128)(2,1)S(1)}, bf16[8,1024,256]{2,1,0:T(8,128)(2,1)S(1)}, bf16[8,512,512]{2,1,0:T(8,128)(2,1)S(1)}) custom-call(f32[2,3]{1,0:T(2,128)} %qp_hbm.1, s32[1,3]{1,0:T(1,128)} %rpv_hbm.1, s32[1,1]{1,0:T(1,128)} %bitcast.17.rpw_hbm, bf16[2,1,4,12288]{3,2,1,0:T(4,128)(2,1)} %x_hbm.1, ...), custom_call_target="tpu_custom_call" | custom-call | tf_op jit(solution)/shard_map/pallas_call | solution.py:524
  22.4 6.3 %shard_map.119 = bf16[128,48,128]{2,1,0:T(8,128)(2,1)} custom-call(bf16[8,3,1,128,128]{4,3,2,1,0:T(8,128)(2,1)S(1)} %get-tuple-element.8.gath, bf16[8,1024,256]{2,1,0:T(8,128)(2,1)S(1)} %get-tuple-element.9.gs, bf16[8,512,512]{2,1,0:T(8,128)(2,1)S(1)} %get-tuple-element.10.vb), custom_call_target="tpu_custom_call" | custom-call | tf_op jit(solution)/shard_map/pallas_call | solution.py:559

commit v4 on v3

--- a/solution.py
+++ b/solution.py
@@ -1,4 +1,5 @@
 import functools
+import math
 
 import jax
 import jax.numpy as jnp
@@ -43,6 +44,73 @@
         tiles = turned
         bit *= 2
     return [t if i == 0 else pltpu.roll(t, shape[axis] - i * unit, axis) for i, t in enumerate(tiles)]
+
+
+def cell_sum(t, sets, gath, gs):
+    chunks, _, groups = gath.shape[:3]
+    left = jnp.concatenate(
+        [jnp.concatenate([gath[j, i, g] for j in range(chunks) for g in range(groups)], axis=1) for i in sets],
+        axis=0,
+    )
+    blocks = gs.shape[0] // 2
+    return tuple(dot(left, gs[c * blocks + t]).astype(bf16) for c in range(2))
+
+
+def finish(t, field, modes, q_count, bands, octets, rest, gs, vb, rt, scr):
+    blocks = gs.shape[0] // 2
+    near = gs.shape[2] // LANES
+    span = LANES // bands
+    halves = bands * bands // LANES
+    quad = 16 // (halves * q_count)
+    many = span // quad
+    k_count = near * blocks * span
+    last = modes // 8 * q_count
+    sets = [j * q_count + q for j in octets for q in range(q_count)] + ([last] if rest else [])
+    for c in range(2):
+        for o in range(near):
+            for n in range(len(sets)):
+                tiles = []
+                for i in range(8):
+                    at = (n * 8 + i) * bands
+                    tiles.append(field[c][at : at + bands, o * LANES : (o + 1) * LANES])
+                for i, tile in enumerate(exchange(tiles, bands)):
+                    at = (c * span + i) * bands
+                    rt[o, n, at : at + bands, :] = tile
+    turn = iota((16, LANES), 0) & (q_count - 1)
+
+    def choose(tiles):
+        tile = tiles[0]
+        for q in range(1, q_count):
+            tile = jnp.where(turn == q, tiles[q], tile)
+        return tile
+
+    for o in range(near):
+        right = jnp.concatenate([rt[o, n] for n in range(len(sets))], axis=1)
+        done = dot(vb[t * near + o], right)
+        for c in range(2):
+            for g in range(many):
+                base = (c * many + g) * span * 16
+
+                def tile(n, i):
+                    at = base + i * 16
+                    return done[at : at + 16, n * LANES : (n + 1) * LANES].astype(bf16)
+
+                found = []
+                for j in range(len(octets)):
+                    found += exchange(
+                        [choose([tile(j * q_count + q, i) for q in range(q_count)]) for i in range(span)], bands
+                    )
+                if rest:
+                    tiles = exchange([tile(len(sets) - 1, i) for i in range(span)], bands)
+                    found += [choose([tiles[q * rest + i] for q in range(q_count)]) for i in range(rest)]
+                for m in range(0, len(found), quad):
+                    tiles = (found[m : m + quad] + [None] * quad)[:quad]
+                    tiles = exchange(tiles, halves * q_count, 0)
+                    at = m * halves * q_count
+                    tall = min(quad, len(found) - m) * halves * q_count
+                    for i in range(quad):
+                        k = (t * near + o) * span + g * quad + i
+                        scr[c * k_count + k, at : at + tall, :] = tiles[i][:tall]
 
 
 def gather_kernel(
@@ -84,6 +152,7 @@
     turned,
     p2,
     u2,
+    v2,
     loads,
     lat_send,
     lat_recv,
@@ -149,17 +218,17 @@
         wr = pr * mr - pi * mi
         wi = pr * mi + pi * mr
         for d in range(lat_count):
-            done = 0
-            while done < modes:
-                first_row = q * modes + done
-                take = min(8 - first_row % 8, modes - done)
-                rows = slice(d * modes + done, d * modes + done + take)
-                at = d * 2 * qn + first_row // 8 * 16 + first_row % 8
+            rest = modes % 8
+            for n in range(0, modes, 8):
+                take = min(8, modes - n)
+                rows = slice(d * modes + n, d * modes + n + take)
+                at = d * 2 * qn + (n // 8 * q_count + q) * 16
+                if take == rest:
+                    at = d * 2 * qn + n // 8 * q_count * 16 + q * rest
                 wre[at : at + take, :] = wr[rows]
                 wim[at : at + take, :] = -wi[rows]
                 wre[at + 8 : at + 8 + take, :] = wi[rows]
                 wim[at + 8 : at + 8 + take, :] = wr[rows]
-                done += take
 
     for c in range(2):
         x = x_ref[c, 0].astype(f32)
@@ -257,31 +326,30 @@
     lax.fori_loop(0, cells, grow, 0)
 
     tall = 2 * bands * span * q_count
-    height = span // quad * halves * q_count * quad
-    row = iota((tall, LANES), 0)
-    at_q = row & (q_count - 1)
-    at_k = ((row // (quad * halves * q_count)) & (span // quad - 1)) * quad + (
-        (row // (halves * q_count)) & (quad - 1)
-    )
-    same = [(at_k == iota((tall, LANES), 1) // bands) & (at_q == q) for q in range(q_count)]
-    row = iota((tall, 2 * bands), 0)
-    band = ((row // q_count) & (halves - 1)) * span + ((row // height) & (span - 1))
-    band = band + row // (tall // 2) * bands
-    repeat = (band == iota((tall, 2 * bands), 1)).astype(f32).astype(bf16)
-
-    def lay(q):
-        keep = jnp.concatenate([mkq_ref[q].astype(f32)] * bands, axis=0)
-        turn = []
-        for c in range(2):
-            wide = dot((v_ref[c, q].astype(f32) * keep).astype(bf16), spread)
-            turn.append(dot(take_minor, jnp.where(major, wide, 0.0).astype(bf16)))
+
+    def lay(stage):
+        if stage == 0:
+            for q in range(q_count):
+                keep = jnp.concatenate([mkq_ref[q].astype(f32)] * bands, axis=0)
+                turn = []
+                for c in range(2):
+                    wide = dot((v_ref[c, q].astype(f32) * keep).astype(bf16), spread)
+                    turn.append(dot(take_minor, jnp.where(major, wide, 0.0).astype(bf16)).astype(bf16))
+                at = q * 2 * bands
+                v2[0, at : at + bands, :], v2[0, at + bands : at + 2 * bands, :] = turn[0], -turn[1]
+                v2[1, at : at + bands, :], v2[1, at + bands : at + 2 * bands, :] = turn[1], turn[0]
+            return
+        row = iota((tall, LANES), 0)
+        at_k = ((row // (span * 16)) & (span // quad - 1)) * quad + ((row // (halves * q_count)) & (quad - 1))
+        same = at_k == iota((tall, LANES), 1) // bands
+        row = iota((tall, q_count * 2 * bands), 0)
+        band = ((row // q_count) & (halves - 1)) * span + ((row // 16) & (span - 1))
+        band = ((row & (q_count - 1)) * 2 + row // (tall // 2)) * bands + band
+        repeat = (band == iota((tall, q_count * 2 * bands), 1)).astype(f32).astype(bf16)
         for o in range(k_count // span):
-            re, im = (x[:, o * LANES : (o + 1) * LANES] for x in turn)
-            both = [jnp.concatenate([re, -im], axis=0), jnp.concatenate([im, re], axis=0)]
             for c in range(2):
-                wide = jnp.where(same[q], dot(repeat, both[c].astype(bf16)), 0.0)
-                at = (q * 2 + c) * LANES
-                vb[o, :, at : at + LANES] = wide.astype(bf16)
+                wide = dot(repeat, v2[c, :, o * LANES : (o + 1) * LANES])
+                vb[o, :, c * LANES : (c + 1) * LANES] = jnp.where(same, wide, 0.0).astype(bf16)
 
     def relayed(source, target):
         if chips < 3:
@@ -360,17 +428,18 @@
     waits = sorted(
         ((i + min(step, 1) + 0.1 * step, step, i) for step in range(chips - 1) for i in range(sets))
     )
-    laid = 0
+    stage = 0
     for _, step, i in waits:
         source = apart(step)
         over(2 * source + core, i, pair, chip_send.at[i, 0], chip_recv.at[i, source]).wait_recv()
         onward(i, source, start)
         pass_on(2 * source + core, i, step)
-        if i == 0 and step != 1 and laid < q_count:
-            lay(laid)
-            laid += 1
-    for q in range(laid, q_count):
-        lay(q)
+        if stage < 2 and i == 0 and step != 1:
+            lay(stage)
+            stage += 1
+    while stage < 2:
+        lay(stage)
+        stage += 1
     for copy in third:
         copy.wait_recv()
     for copies in first:
@@ -386,74 +455,27 @@
 
 def couple_kernel(modes, q_count, bands, gath, gs, vb, out_ref, rt, scr, sems):
     blocks = gs.shape[0] // 2
+    span = LANES // bands
     near = gs.shape[2] // LANES
-    span = LANES // bands
-    width = bands * bands
-    halves = width // LANES
-    octets = -(-modes // span)
-    quad = 16 // (halves * q_count)
-    many = span // quad
     k_count = near * blocks * span
-    held = modes * halves * q_count
+    held = out_ref.shape[1]
+    sets = range(gath.shape[1])
 
     def leave(t):
         copies = []
         for c in range(2):
             rows = pl.ds(c * k_count + t * near * span, near * span)
-            copies.append(
-                pltpu.make_async_copy(scr.at[rows, :held], out_ref.at[rows], sems.at[t, c])
-            )
+            copies.append(pltpu.make_async_copy(scr.at[rows, :held], out_ref.at[rows], sems.at[t, c]))
         return copies
 
-    def finish(t, carry):
-        chunks, sets, groups = gath.shape[:3]
-        left = jnp.concatenate(
-            [
-                jnp.concatenate([gath[j, i, g] for j in range(chunks) for g in range(groups)], axis=1)
-                for i in range(sets)
-            ],
-            axis=0,
-        )
-        field = [dot(left, gs[c * blocks + t]).astype(bf16) for c in range(2)]
-        for o in range(near):
-            for q in range(q_count):
-                for c in range(2):
-                    for s in range(octets):
-                        tiles = []
-                        for i in range(span):
-                            m = s * span + i
-                            at = (q * modes + m) * bands
-                            tiles.append(
-                                field[c][at : at + bands, o * LANES : (o + 1) * LANES] if m < modes else None
-                            )
-                        tiles = exchange(tiles, bands)
-                        for i in range(span):
-                            at = ((q * 2 + c) * span + i) * bands
-                            rt[o, s, at : at + bands, :] = tiles[i]
-            right = jnp.concatenate([rt[o, s] for s in range(octets)], axis=1)
-            done = dot(vb[t * near + o], right)
-            for c in range(2):
-                for g in range(many):
-                    found = []
-                    for s in range(octets):
-                        tiles = []
-                        for i in range(span):
-                            at = ((c * span + i) * many + g) * 16
-                            tiles.append(done[at : at + 16, s * LANES : (s + 1) * LANES].astype(bf16))
-                        found += exchange(tiles, bands)
-                    for m in range(0, modes, quad):
-                        tiles = [found[i] if i < modes else None for i in range(m, m + quad)]
-                        tiles = exchange(tiles, halves * q_count, 0)
-                        tall = min(quad, modes - m) * halves * q_count
-                        for i in range(quad):
-                            k = (t * near + o) * span + g * quad + i
-                            at = m * halves * q_count
-                            scr[c * k_count + k, at : at + tall, :] = tiles[i][:tall]
+    def step(t, field):
+        ahead = cell_sum(jnp.minimum(t + 1, blocks - 1), sets, gath, gs)
+        finish(t, field, modes, q_count, bands, range(modes // 8), modes % 8, gs, vb, rt, scr)
         for copy in leave(t):
             copy.start()
-        return carry
-
-    lax.fori_loop(0, blocks, finish, 0)
+        return ahead
+
+    lax.fori_loop(0, blocks, step, cell_sum(0, sets, gath, gs))
     for t in range(blocks):
         for copy in leave(t):
             copy.wait()
@@ -484,7 +506,7 @@
     modes = mode_count // lat_count
     cells = re_vectors.shape[0]
     span = LANES // bands
-    qn = up(q_count * modes, 8)
+    qn = modes // 8 * 8 * q_count + up(modes % 8 * q_count, 8)
     sets = qn // 8
     groups = local // (span // 2)
     octets = -(-modes // span)
@@ -516,20 +538,19 @@
         keep_k,
         keep_kq,
     )
-    kept = (
-        2 * kpt_count * sets * groups * 8 * bands * LANES
-        + 2 * 2 * blocks * 2 * cells * bands * lanes
-        + 2 * (k_count // span) * tall * q_count * 2 * LANES
-    )
+    count = modes * (width // LANES)
+    held = count * q_count
+    shapes = [
+        ((kpt_count, sets, groups, 8 * bands, LANES), bf16),
+        ((2 * blocks, 2 * cells * bands, lanes), bf16),
+        ((k_count // span, tall, 2 * LANES), bf16),
+    ]
+    kept = sum(2 * math.prod(shape) for shape, _ in shapes)
     parts = pl.pallas_call(
         functools.partial(gather_kernel, lat_count, kpt_count, modes),
         in_specs=[anywhere] * len(inputs),
-        out_specs=[vmem] * 3,
-        out_shape=[
-            pltpu.VMEM((kpt_count, sets, groups, 8 * bands, LANES), bf16),
-            pltpu.VMEM((2 * blocks, 2 * cells * bands, lanes), bf16),
-            pltpu.VMEM((k_count // span, tall, q_count * 2 * LANES), bf16),
-        ],
+        out_specs=[vmem] * len(shapes),
+        out_shape=[pltpu.VMEM(shape, dtype) for shape, dtype in shapes],
         scratch_shapes=[pltpu.VMEM(x.shape, x.dtype) for x in inputs]
         + [
             pltpu.VMEM((2 * local * mode_count * (width // LANES), LANES), f32),
@@ -540,6 +561,7 @@
             pltpu.VMEM((8 * bands, LANES), f32),
             pltpu.VMEM((2, cells, bands * k_count), f32),
             pltpu.VMEM((2, bands, bands * k_count), f32),
+            pltpu.VMEM((2, q_count * 2 * bands, bands * k_count), bf16),
             dma((len(inputs),)),
             dma((sets, lat_count)),
             dma((sets, lat_count)),
@@ -553,16 +575,14 @@
             collective_id=0, has_side_effects=True, vmem_limit_bytes=63 * 1024 * 1024 - kept
         ),
     )(*inputs)
-    count = modes * (width // LANES)
-    held = count * q_count
     result = jax.ShapeDtypeStruct((2 * k_count, held, LANES), bf16)
     out = pl.pallas_call(
         functools.partial(couple_kernel, modes, q_count, bands),
-        in_specs=[vmem] * 3,
+        in_specs=[vmem] * len(parts),
         out_specs=anywhere,
         out_shape=result,
         scratch_shapes=[
-            pltpu.VMEM((lanes // LANES, octets, q_count * 2 * LANES, LANES), bf16),
+            pltpu.VMEM((lanes // LANES, sets, 2 * LANES, LANES), bf16),
             pltpu.VMEM((2 * k_count, up(held, 16), LANES), bf16),
             dma((blocks, 2)),
         ],

time: 28.8 us -> 27.5 us (0.955)
  Pallas kernels: 28 us -> 26.7 us
    pallas_call x1, Pallas kernels: 6.27 us -> 5.58 us  [per_device(): pl.pallas_call(functools.partial(couple_kernel, modes, q_count, bands), i...]
    pallas_call x1, Pallas kernels: 21.8 us -> 21.1 us  [per_device(): pl.pallas_call(functools.partial(gather_kernel, lat_count, kpt_count, mod...]
where the time goes in v4:
time: 27.5 us; the launch traced here: 27.4 us
  Pallas kernels  26.7 us (97%)
  between operations  0.66 us (2%)
    pallas_call x1, Pallas kernels, per_device(): pl.pallas_call(functools.partial(gather_kernel, lat_count, kpt_count, mod...  21.1 us
    pallas_call x1, Pallas kernels, per_device(): pl.pallas_call(functools.partial(couple_kernel, modes, q_count, bands), i...  5.58 us

profile of v4, /device:TPU:0, one launch (start us, length us, event | category | flops | bytes accessed | tf_op | source)
XLA Modules:
  0.0 27.4 jit_solution(7912372026726266171)
XLA Ops:
  0.7 21.1 %shard_map.118 = (bf16[8,3,1,128,128]{4,3,2,1,0:T(8,128)(2,1)S(1)}, bf16[8,1024,256]{2,1,0:T(8,128)(2,1)S(1)}, bf16[8,512,256]{2,1,0:T(8,128)(2,1)S(1)}) custom-call(f32[2,3]{1,0:T(2,128)} %qp_hbm.1, s32[1,3]{1,0:T(1,128)} %rpv_hbm.1, s32[1,1]{1,0:T(1,128)} %bitcast.17.rpw_hbm, bf16[2,1,4,12288]{3,2,1,0:T(4,128)(2,1)} %x_hbm.1, ...), custom_call_target="tpu_custom_call" | custom-call | tf_op jit(solution)/shard_map/pallas_call | solution.py:549
  21.8 5.6 %shard_map.119 = bf16[128,48,128]{2,1,0:T(8,128)(2,1)} custom-call(bf16[8,3,1,128,128]{4,3,2,1,0:T(8,128)(2,1)S(1)} %get-tuple-element.8.gath, bf16[8,1024,256]{2,1,0:T(8,128)(2,1)S(1)} %get-tuple-element.9.gs, bf16[8,512,256]{2,1,0:T(8,128)(2,1)S(1)} %get-tuple-element.10.vb), custom_call_target="tpu_custom_call" | custom-call | tf_op jit(solution)/shard_map/pallas_call | solution.py:579

commit v5 on v4

--- a/solution.py
+++ b/solution.py
@@ -46,14 +46,26 @@
     return [t if i == 0 else pltpu.roll(t, shape[axis] - i * unit, axis) for i, t in enumerate(tiles)]
 
 
-def cell_sum(t, sets, gath, gs):
-    chunks, _, groups = gath.shape[:3]
+def apart(chip, chips, step):
+    found = 0
+    for z in range(chips):
+        others = sorted((o for o in range(chips) if o != z), key=lambda o: abs(o - z))
+        found = found + jnp.where(chip == z, others[step], 0)
+    return found
+
+
+def cell_sum(t, some, gath, gs):
+    _, sets, groups = gath.shape[:3]
+    deep = 2 * groups * LANES
     left = jnp.concatenate(
-        [jnp.concatenate([gath[j, i, g] for j in range(chunks) for g in range(groups)], axis=1) for i in sets],
+        [
+            jnp.concatenate([gath[2 * z + c, i, g] for z in some for c in range(2) for g in range(groups)], axis=1)
+            for i in range(sets)
+        ],
         axis=0,
     )
-    blocks = gs.shape[0] // 2
-    return tuple(dot(left, gs[c * blocks + t]).astype(bf16) for c in range(2))
+    right = [gs[t, pl.ds(pl.multiple_of(z * deep, deep), deep), :] for z in some]
+    return dot(left, jnp.concatenate(right, axis=0))
 
 
 def finish(t, field, modes, q_count, bands, octets, rest, gs, vb, rt, scr):
@@ -132,6 +144,7 @@
     gath,
     gs,
     vb,
+    acc,
     qp,
     rpv,
     rpw,
@@ -158,7 +171,6 @@
     lat_recv,
     chip_send,
     chip_recv,
-    relay_send,
     pair_send,
     pair_recv,
 ):
@@ -351,20 +363,6 @@
                 wide = dot(repeat, v2[c, :, o * LANES : (o + 1) * LANES])
                 vb[o, :, c * LANES : (c + 1) * LANES] = jnp.where(same, wide, 0.0).astype(bf16)
 
-    def relayed(source, target):
-        if chips < 3:
-            return False
-        return ((target == chips - 1) & (source == chips - 3)) | ((target == 0) & (source == 2))
-
-    def apart(step):
-        found = 0
-        for z in range(chips):
-            others = [o for o in range(chips) if o != z]
-            between = {1: 2, chips - 2: chips - 3}.get(z) if chips > 2 else None
-            others = sorted(others, key=lambda o: (abs(o - z), o != between))
-            found = found + jnp.where(chip == z, others[step], 0)
-        return found
-
     def over(source, i, target, send_sem, recv_sem):
         return pltpu.make_async_remote_copy(
             src_ref=gath.at[source, i],
@@ -377,21 +375,11 @@
 
     def outward(i, act):
         for down in (True, False):
-            for z in reversed(range(chips)) if down else range(chips):
-                ahead = (chip < z) if down else (chip > z)
-
-                @pl.when(ahead & jnp.logical_not(relayed(chip, z)))
+            for z in range(chips) if down else reversed(range(chips)):
+
+                @pl.when((chip > z) if down else (chip < z))
                 def _():
                     act(over(kpt, i, 2 * z + core, chip_send.at[i, z], chip_recv.at[i, chip]))
-
-    def onward(i, source, act):
-        for n, (at, end, origin) in enumerate(((chips - 2, chips - 1, chips - 3), (1, 0, 2))):
-            if chips < 3:
-                continue
-
-            @pl.when((chip == at) & (source == origin))
-            def _():
-                act(over(2 * source + core, i, 2 * end + core, relay_send.at[i, n], chip_recv.at[i, source]))
 
     def start(copy):
         copy.start()
@@ -404,7 +392,14 @@
     def pass_on(source, i, step):
         copy = over(source, i, pair, pair_send.at[i, step], pair_recv.at[i, step])
         copy.start()
-        third.append(copy)
+        third.append((copy, step))
+
+    def begin(near):
+        for copy, step in third:
+            if step in (0, chips - 1):
+                copy.wait_recv()
+        for t in range(2 * blocks):
+            acc[t] = cell_sum(t, [chip, near], gath, gs)
 
     cut = span // 2
     for i in range(sets):
@@ -425,41 +420,51 @@
         outward(i, start)
         pass_on(kpt, i, chips - 1)
 
+    nearest = [apart(chip, chips, step) for step in range(chips - 1)]
     waits = sorted(
         ((i + min(step, 1) + 0.1 * step, step, i) for step in range(chips - 1) for i in range(sets))
     )
+    ready = [n for n, (_, step, _) in enumerate(waits) if step == 0][-1] + 2
     stage = 0
-    for _, step, i in waits:
-        source = apart(step)
-        over(2 * source + core, i, pair, chip_send.at[i, 0], chip_recv.at[i, source]).wait_recv()
-        onward(i, source, start)
-        pass_on(2 * source + core, i, step)
-        if stage < 2 and i == 0 and step != 1:
+    for n, (_, step, i) in enumerate(waits):
+        if stage < 2 and n in (1, 3):
             lay(stage)
             stage += 1
+        if n == ready:
+            begin(nearest[0])
+        source = nearest[step]
+        over(2 * source + core, i, pair, chip_send.at[i, 0], chip_recv.at[i, source]).wait_recv()
+        pass_on(2 * source + core, i, step)
     while stage < 2:
         lay(stage)
         stage += 1
-    for copy in third:
-        copy.wait_recv()
+    if ready >= len(waits):
+        begin(nearest[0])
+    for copy, step in third:
+        if 0 < step < chips - 1:
+            copy.wait_recv()
     for copies in first:
         for copy in copies:
             copy.wait_send()
-    for copy in third:
+    for copy, _ in third:
         copy.wait_send()
     for i in range(sets):
         outward(i, sent)
-        for step in range(chips - 1):
-            onward(i, apart(step), sent)
-
-
-def couple_kernel(modes, q_count, bands, gath, gs, vb, out_ref, rt, scr, sems):
+
+
+def couple_kernel(modes, q_count, bands, gath, gs, vb, acc, out_ref, rt, scr, sems):
     blocks = gs.shape[0] // 2
     span = LANES // bands
     near = gs.shape[2] // LANES
     k_count = near * blocks * span
     held = out_ref.shape[1]
-    sets = range(gath.shape[1])
+    chips = gath.shape[0] // 2
+    rest = [apart(lax.axis_index("kpt") // 2, chips, step) for step in range(1, chips - 1)]
+
+    def total(t):
+        return tuple(
+            (acc[c * blocks + t] + cell_sum(c * blocks + t, rest, gath, gs)).astype(bf16) for c in range(2)
+        )
 
     def leave(t):
         copies = []
@@ -469,13 +474,13 @@
         return copies
 
     def step(t, field):
-        ahead = cell_sum(jnp.minimum(t + 1, blocks - 1), sets, gath, gs)
+        ahead = total(jnp.minimum(t + 1, blocks - 1))
         finish(t, field, modes, q_count, bands, range(modes // 8), modes % 8, gs, vb, rt, scr)
         for copy in leave(t):
             copy.start()
         return ahead
 
-    lax.fori_loop(0, blocks, step, cell_sum(0, sets, gath, gs))
+    lax.fori_loop(0, blocks, step, total(0))
     for t in range(blocks):
         for copy in leave(t):
             copy.wait()
@@ -513,7 +518,7 @@
     chips = kpt_count // 2
     lanes = 2 * LANES
     blocks = bands * k_count // lanes
-    assert coarse.shape[1] == 1 and local % (span // 2) == 0 and bands & (bands - 1) == 0
+    assert chips > 2 and coarse.shape[1] == 1 and local % (span // 2) == 0 and bands & (bands - 1) == 0
 
     uk = jnp.transpose(u_k, (0, 2, 3, 1)).reshape(2, width, k_count)
     ukq = jnp.transpose(u_kq, (0, 1, 3, 4, 2)).reshape(2, q_count, width, k_count)
@@ -544,8 +549,9 @@
         ((kpt_count, sets, groups, 8 * bands, LANES), bf16),
         ((2 * blocks, 2 * cells * bands, lanes), bf16),
         ((k_count // span, tall, 2 * LANES), bf16),
+        ((2 * blocks, qn * bands, lanes), f32),
     ]
-    kept = sum(2 * math.prod(shape) for shape, _ in shapes)
+    kept = sum(4 * math.prod(shape) for shape, _ in shapes[3:]) + sum(2 * math.prod(shape) for shape, _ in shapes[:3])
     parts = pl.pallas_call(
         functools.partial(gather_kernel, lat_count, kpt_count, modes),
         in_specs=[anywhere] * len(inputs),
@@ -567,7 +573,6 @@
             dma((sets, lat_count)),
             dma((sets, chips)),
             dma((sets, chips)),
-            dma((sets, 2)),
             dma((sets, chips)),
             dma((sets, chips)),
         ],

time: 27.5 us -> 26 us (0.945)
  Pallas kernels: 26.7 us -> 25.2 us
    pallas_call x1, Pallas kernels: 21.1 us -> 20.4 us  [per_device(): pl.pallas_call(functools.partial(gather_kernel, lat_count, kpt_count, mod...]
    pallas_call x1, Pallas kernels: 5.58 us -> 4.83 us  [per_device(): pl.pallas_call(functools.partial(couple_kernel, modes, q_count, bands), i...]
where the time goes in v5:
time: 26 us; the launch traced here: 25.8 us
  Pallas kernels  25.2 us (97%)
  between operations  0.66 us (3%)
    pallas_call x1, Pallas kernels, per_device(): pl.pallas_call(functools.partial(gather_kernel, lat_count, kpt_count, mod...  20.4 us
    pallas_call x1, Pallas kernels, per_device(): pl.pallas_call(functools.partial(couple_kernel, modes, q_count, bands), i...  4.83 us

profile of v5, /device:TPU:0, one launch (start us, length us, event | category | flops | bytes accessed | tf_op | source)
XLA Modules:
  0.0 25.8 jit_solution(7692793307620126347)
XLA Ops:
  0.7 20.4 %shard_map.118 = (bf16[8,3,1,128,128]{4,3,2,1,0:T(8,128)(2,1)S(1)}, bf16[8,1024,256]{2,1,0:T(8,128)(2,1)S(1)}, bf16[8,512,256]{2,1,0:T(8,128)(2,1)S(1)}, f32[8,384,256]{2,1,0:T(8,128)S(1)}) custom-call(f32[2,3]{1,0:T(2,128)} %qp_hbm.1, s32[1,3]{1,0:T(1,128)} %rpv_hbm.1, s32[1,1]{1,0:T(1,128)} %bitcast.17.rpw_hbm, bf16[2,1,4,12288]{3,2,1,0:T(4,128)(2,1)} %x_hbm.1, ...), custom_call_target="tpu_custom_call" | custom-call | tf_op jit(solution)/shard_map/pallas_call | solution.py:555
  21.0 4.8 %shard_map.119 = bf16[128,48,128]{2,1,0:T(8,128)(2,1)} custom-call(bf16[8,3,1,128,128]{4,3,2,1,0:T(8,128)(2,1)S(1)} %get-tuple-element.9.gath, bf16[8,1024,256]{2,1,0:T(8,128)(2,1)S(1)} %get-tuple-element.10.gs, bf16[8,512,256]{2,1,0:T(8,128)(2,1)S(1)} %get-tuple-element.11.vb, f32[8,384,256]{2,1,0:T(8,128)S(1)} %get-tuple-element.12.acc), custom_call_target="tpu_custom_call" | custom-call | tf_op jit(solution)/shard_map/pallas_call | solution.py:584

commit v6 on v5

--- a/solution.py
+++ b/solution.py
@@ -474,13 +474,15 @@
         return copies
 
     def step(t, field):
-        ahead = total(jnp.minimum(t + 1, blocks - 1))
+        ahead = total(t + 1) if t + 1 < blocks else None
         finish(t, field, modes, q_count, bands, range(modes // 8), modes % 8, gs, vb, rt, scr)
         for copy in leave(t):
             copy.start()
         return ahead
 
-    lax.fori_loop(0, blocks, step, total(0))
+    field = total(0)
+    for t in range(blocks):
+        field = step(t, field)
     for t in range(blocks):
         for copy in leave(t):
             copy.wait()

time: 26 us -> 24.6 us (0.946)
  Pallas kernels: 25.2 us -> 23.8 us
    pallas_call x1, Pallas kernels: 4.83 us -> 3.42 us  [per_device(): pl.pallas_call(functools.partial(couple_kernel, modes, q_count, bands), i...]
where the time goes in v6:
time: 24.6 us; the launch traced here: 24.4 us
  Pallas kernels  23.8 us (97%)
  between operations  0.66 us (3%)
    pallas_call x1, Pallas kernels, per_device(): pl.pallas_call(functools.partial(gather_kernel, lat_count, kpt_count, mod...  20.4 us
    pallas_call x1, Pallas kernels, per_device(): pl.pallas_call(functools.partial(couple_kernel, modes, q_count, bands), i...  3.42 us

profile of v6, /device:TPU:0, one launch (start us, length us, event | category | flops | bytes accessed | tf_op | source)
XLA Modules:
  0.0 24.4 jit_solution(6693256070346205680)
XLA Ops:
  0.7 20.4 %shard_map.118 = (bf16[8,3,1,128,128]{4,3,2,1,0:T(8,128)(2,1)S(1)}, bf16[8,1024,256]{2,1,0:T(8,128)(2,1)S(1)}, bf16[8,512,256]{2,1,0:T(8,128)(2,1)S(1)}, f32[8,384,256]{2,1,0:T(8,128)S(1)}) custom-call(f32[2,3]{1,0:T(2,128)} %qp_hbm.1, s32[1,3]{1,0:T(1,128)} %rpv_hbm.1, s32[1,1]{1,0:T(1,128)} %bitcast.17.rpw_hbm, bf16[2,1,4,12288]{3,2,1,0:T(4,128)(2,1)} %x_hbm.1, ...), custom_call_target="tpu_custom_call" | custom-call | tf_op jit(solution)/shard_map/pallas_call | solution.py:557
  21.0 3.4 %shard_map.119 = bf16[128,48,128]{2,1,0:T(8,128)(2,1)} custom-call(bf16[8,3,1,128,128]{4,3,2,1,0:T(8,128)(2,1)S(1)} %get-tuple-element.9.gath, bf16[8,1024,256]{2,1,0:T(8,128)(2,1)S(1)} %get-tuple-element.10.gs, bf16[8,512,256]{2,1,0:T(8,128)(2,1)S(1)} %get-tuple-element.11.vb, f32[8,384,256]{2,1,0:T(8,128)S(1)} %get-tuple-element.12.acc), custom_call_target="tpu_custom_call" | custom-call | tf_op jit(solution)/shard_map/pallas_call | solution.py:586

commit v7 on v6

--- a/solution.py
+++ b/solution.py
@@ -56,19 +56,19 @@
 
 def cell_sum(t, some, gath, gs):
     _, sets, groups = gath.shape[:3]
-    deep = 2 * groups * LANES
+    deep = groups * LANES
     left = jnp.concatenate(
         [
-            jnp.concatenate([gath[2 * z + c, i, g] for z in some for c in range(2) for g in range(groups)], axis=1)
+            jnp.concatenate([gath[j, i, g] for j in some for g in range(groups)], axis=1)
             for i in range(sets)
         ],
         axis=0,
     )
-    right = [gs[t, pl.ds(pl.multiple_of(z * deep, deep), deep), :] for z in some]
+    right = [gs[t, pl.ds(pl.multiple_of(j * deep, deep), deep), :] for j in some]
     return dot(left, jnp.concatenate(right, axis=0))
 
 
-def finish(t, field, modes, q_count, bands, octets, rest, gs, vb, rt, scr):
+def finish(t, field, modes, q_count, bands, octets, rest, gs, vb, rt, scr, leave):
     blocks = gs.shape[0] // 2
     near = gs.shape[2] // LANES
     span = LANES // bands
@@ -123,6 +123,8 @@
                     for i in range(quad):
                         k = (t * near + o) * span + g * quad + i
                         scr[c * k_count + k, at : at + tall, :] = tiles[i][:tall]
+        for copy in leave(t * near + o):
+            copy.start()
 
 
 def gather_kernel(
@@ -179,6 +181,7 @@
     load = []
     for i in range(len(given)):
         load.append(pltpu.make_async_copy(given[i], held[i], loads.at[i]))
+    for i in (3, 4, 0, 1, 2, *range(5, len(given))):
         load[i].start()
     lat = lax.axis_index("lat")
     kpt = lax.axis_index("kpt")
@@ -234,9 +237,9 @@
             for n in range(0, modes, 8):
                 take = min(8, modes - n)
                 rows = slice(d * modes + n, d * modes + n + take)
-                at = d * 2 * qn + (n // 8 * q_count + q) * 16
+                at = ((n // 8 * q_count + q) * lat_count + d) * 16
                 if take == rest:
-                    at = d * 2 * qn + n // 8 * q_count * 16 + q * rest
+                    at = (n // 8 * q_count * lat_count + d) * 16 + q * rest
                 wre[at : at + take, :] = wr[rows]
                 wim[at : at + take, :] = -wi[rows]
                 wre[at + 8 : at + 8 + take, :] = wi[rows]
@@ -259,15 +262,6 @@
             axis=1,
         ).astype(bf16)
 
-    left, right = wre[...].astype(bf16), wim[...].astype(bf16)
-    for e in range(local):
-        piece = (dot(left, rows_of(0, e)) + dot(right, rows_of(1, e))).astype(bf16)
-        for d in range(lat_count):
-            for i in range(sets):
-                at = d * 2 * qn + i * 16
-                part[i, d, e] = piece[at : at + 16]
-
-    pl.semaphore_wait(barrier, lat_count + chips - 1)
     first = [
         [
             pltpu.make_async_remote_copy(
@@ -282,8 +276,17 @@
         ]
         for i in range(sets)
     ]
-    for copies in first:
-        for copy in copies:
+    field = [[rows_of(c, e) for e in range(local)] for c in range(2)]
+    for i in range(sets):
+        cut = slice(i * lat_count * 16, (i + 1) * lat_count * 16)
+        left, right = wre[cut, :].astype(bf16), wim[cut, :].astype(bf16)
+        for e in range(local):
+            piece = (dot(left, field[0][e]) + dot(right, field[1][e])).astype(bf16)
+            for d in range(lat_count):
+                part[i, d, e] = piece[d * 16 : (d + 1) * 16]
+        if i == 0:
+            pl.semaphore_wait(barrier, lat_count + chips - 1)
+        for copy in first[i]:
             copy.start()
 
     for copy in load[5:]:
@@ -374,8 +377,8 @@
         )
 
     def outward(i, act):
-        for down in (True, False):
-            for z in range(chips) if down else reversed(range(chips)):
+        for down, some in ((True, [0]), (False, reversed(range(chips))), (True, range(1, chips))):
+            for z in some:
 
                 @pl.when((chip > z) if down else (chip < z))
                 def _():
@@ -399,7 +402,7 @@
             if step in (0, chips - 1):
                 copy.wait_recv()
         for t in range(2 * blocks):
-            acc[t] = cell_sum(t, [chip, near], gath, gs)
+            acc[t] = cell_sum(t, [2 * z + c for z in (chip, near) for c in range(2)], gath, gs)
 
     cut = span // 2
     for i in range(sets):
@@ -424,7 +427,7 @@
     waits = sorted(
         ((i + min(step, 1) + 0.1 * step, step, i) for step in range(chips - 1) for i in range(sets))
     )
-    ready = [n for n, (_, step, _) in enumerate(waits) if step == 0][-1] + 2
+    ready = [n for n, (_, step, _) in enumerate(waits) if step == 0][-1] + 1
     stage = 0
     for n, (_, step, i) in enumerate(waits):
         if stage < 2 and n in (1, 3):
@@ -440,6 +443,9 @@
         stage += 1
     if ready >= len(waits):
         begin(nearest[0])
+    straight = [2 * z + core for z in nearest[1:]]
+    for t in range(2 * blocks):
+        acc[t] += cell_sum(t, straight, gath, gs)
     for copy, step in third:
         if 0 < step < chips - 1:
             copy.wait_recv()
@@ -459,7 +465,8 @@
     k_count = near * blocks * span
     held = out_ref.shape[1]
     chips = gath.shape[0] // 2
-    rest = [apart(lax.axis_index("kpt") // 2, chips, step) for step in range(1, chips - 1)]
+    chip, core = lax.axis_index("kpt") // 2, lax.axis_index("kpt") % 2
+    rest = [2 * apart(chip, chips, step) + 1 - core for step in range(1, chips - 1)]
 
     def total(t):
         return tuple(
@@ -469,21 +476,19 @@
     def leave(t):
         copies = []
         for c in range(2):
-            rows = pl.ds(c * k_count + t * near * span, near * span)
+            rows = pl.ds(c * k_count + t * span, span)
             copies.append(pltpu.make_async_copy(scr.at[rows, :held], out_ref.at[rows], sems.at[t, c]))
         return copies
 
     def step(t, field):
         ahead = total(t + 1) if t + 1 < blocks else None
-        finish(t, field, modes, q_count, bands, range(modes // 8), modes % 8, gs, vb, rt, scr)
-        for copy in leave(t):
-            copy.start()
+        finish(t, field, modes, q_count, bands, range(modes // 8), modes % 8, gs, vb, rt, scr, leave)
         return ahead
 
     field = total(0)
     for t in range(blocks):
         field = step(t, field)
-    for t in range(blocks):
+    for t in range(near * blocks):
         for copy in leave(t):
             copy.wait()
 
@@ -591,7 +596,7 @@
         scratch_shapes=[
             pltpu.VMEM((lanes // LANES, sets, 2 * LANES, LANES), bf16),
             pltpu.VMEM((2 * k_count, up(held, 16), LANES), bf16),
-            dma((blocks, 2)),
+            dma((k_count // span, 2)),
         ],
         compiler_params=pltpu.CompilerParams(vmem_limit_bytes=40 * 1024 * 1024),
     )(*parts)

time: 24.6 us -> 23.7 us (0.963)
  Pallas kernels: 23.8 us -> 22.7 us
    pallas_call x1, Pallas kernels: 20.4 us -> 19.6 us  [per_device(): pl.pallas_call(functools.partial(gather_kernel, lat_count, kpt_count, mod...]
    pallas_call x1, Pallas kernels: 3.42 us -> 3.07 us  [per_device(): pl.pallas_call(functools.partial(couple_kernel, modes, q_count, bands), i...]
where the time goes in v7:
time: 23.7 us; the launch traced here: 23.4 us
  Pallas kernels  22.7 us (96%)
  between operations  0.66 us (3%)
    pallas_call x1, Pallas kernels, per_device(): pl.pallas_call(functools.partial(gather_kernel, lat_count, kpt_count, mod...  19.6 us
    pallas_call x1, Pallas kernels, per_device(): pl.pallas_call(functools.partial(couple_kernel, modes, q_count, bands), i...  3.07 us

profile of v7, /device:TPU:0, one launch (start us, length us, event | category | flops | bytes accessed | tf_op | source)
XLA Modules:
  0.0 23.4 jit_solution(17169309163560977402)
XLA Ops:
  0.7 19.6 %shard_map.118 = (bf16[8,3,1,128,128]{4,3,2,1,0:T(8,128)(2,1)S(1)}, bf16[8,1024,256]{2,1,0:T(8,128)(2,1)S(1)}, bf16[8,512,256]{2,1,0:T(8,128)(2,1)S(1)}, f32[8,384,256]{2,1,0:T(8,128)S(1)}) custom-call(f32[2,3]{1,0:T(2,128)} %qp_hbm.1, s32[1,3]{1,0:T(1,128)} %rpv_hbm.1, s32[1,1]{1,0:T(1,128)} %bitcast.17.rpw_hbm, bf16[2,1,4,12288]{3,2,1,0:T(4,128)(2,1)} %x_hbm.1, ...), custom_call_target="tpu_custom_call" | custom-call | tf_op jit(solution)/shard_map/pallas_call | solution.py:562
  20.3 3.1 %shard_map.119 = bf16[128,48,128]{2,1,0:T(8,128)(2,1)} custom-call(bf16[8,3,1,128,128]{4,3,2,1,0:T(8,128)(2,1)S(1)} %get-tuple-element.9.gath, bf16[8,1024,256]{2,1,0:T(8,128)(2,1)S(1)} %get-tuple-element.10.gs, bf16[8,512,256]{2,1,0:T(8,128)(2,1)S(1)} %get-tuple-element.11.vb, f32[8,384,256]{2,1,0:T(8,128)S(1)} %get-tuple-element.12.acc), custom_call_target="tpu_custom_call" | custom-call | tf_op jit(solution)/shard_map/pallas_call | solution.py:591

commit v8 on v7

--- a/solution.py
+++ b/solution.py
@@ -225,7 +225,7 @@
         term = qp[q : q + 1, :] * rpv[...].astype(f32)
         argument = two_pi * (term[:, 0:1] + term[:, 1:2] + term[:, 2:3])
         argument = jnp.broadcast_to(argument, (1, mode_count))
-        inverse = 1.0 / jnp.broadcast_to(rpw[...].astype(f32), (1, mode_count))
+        inverse = 1.0 / jnp.broadcast_to(rpw[...].astype(f32).reshape(1, 1), (1, mode_count))
         pr = (jnp.cos(argument) * inverse).astype(bf16).astype(f32)
         pi = (jnp.sin(argument) * inverse).astype(bf16).astype(f32)
         mr = rot_ref[0, q].astype(f32).T
@@ -539,7 +539,7 @@
     inputs = (
         q_points,
         rp_vectors,
-        rp_weights.reshape(1, 1),
+        rp_weights,
         coarse,
         modes_rot,
         jnp.transpose(re_vectors),

time: 23.7 us -> 23.7 us (level)
  no operation moved by 1% of the time
where the time goes in v8:
time: 23.7 us; the launch traced here: 23.4 us
  Pallas kernels  22.7 us (96%)
  between operations  0.66 us (3%)
    pallas_call x1, Pallas kernels, per_device(): pl.pallas_call(functools.partial(gather_kernel, lat_count, kpt_count, mod...  19.6 us
    pallas_call x1, Pallas kernels, per_device(): pl.pallas_call(functools.partial(couple_kernel, modes, q_count, bands), i...  3.07 us

profile of v8, /device:TPU:0, one launch (start us, length us, event | category | flops | bytes accessed | tf_op | source)
XLA Modules:
  0.0 23.4 jit_solution(17169309163560977402)
XLA Ops:
  0.7 19.6 %shard_map.118 = (bf16[8,3,1,128,128]{4,3,2,1,0:T(8,128)(2,1)S(1)}, bf16[8,1024,256]{2,1,0:T(8,128)(2,1)S(1)}, bf16[8,512,256]{2,1,0:T(8,128)(2,1)S(1)}, f32[8,384,256]{2,1,0:T(8,128)S(1)}) custom-call(f32[2,3]{1,0:T(2,128)} %qp_hbm.1, s32[1,3]{1,0:T(1,128)} %rpv_hbm.1, s32[1]{0:T(128)S(6)} %copy.14.rpw_hbm, bf16[2,1,4,12288]{3,2,1,0:T(4,128)(2,1)} %x_hbm.1, ...), custom_call_target="tpu_custom_call" | custom-call | tf_op jit(solution)/shard_map/pallas_call | solution.py:562
  20.3 3.1 %shard_map.119 = bf16[128,48,128]{2,1,0:T(8,128)(2,1)} custom-call(bf16[8,3,1,128,128]{4,3,2,1,0:T(8,128)(2,1)S(1)} %get-tuple-element.9.gath, bf16[8,1024,256]{2,1,0:T(8,128)(2,1)S(1)} %get-tuple-element.10.gs, bf16[8,512,256]{2,1,0:T(8,128)(2,1)S(1)} %get-tuple-element.11.vb, f32[8,384,256]{2,1,0:T(8,128)S(1)} %get-tuple-element.12.acc), custom_call_target="tpu_custom_call" | custom-call | tf_op jit(solution)/shard_map/pallas_call | solution.py:591
